TPU v7x, 32 devices: a whole 2x2x4 slice. The times are simulated.
32 devices in a mesh: groups: 2 (over x), seq: 16 (over z, y, core).
Axes of the slice: x: 2, y: 2, z: 4, core: 2. Of those that a mesh axis runs over, the one named last changes fastest.
Arguments:
- prefill_q: bfloat16 [32, 8192], P(('groups', 'seq')), parts along dimension 0, may hold values from -48 to 48
- cache_k: bfloat16 [16384, 1024], P(('groups', 'seq')), parts along dimension 0, may hold values from -4.5 to 4.5
- cache_v: bfloat16 [16384, 1024], P(('groups', 'seq')), parts along dimension 0, may hold values from -4.5 to 4.5
- page_counts: int32 [32], P('groups'), parts along dimension 0, may hold values from 1 to 64, 768 in all
- page_owner: int32 [2048, 1], P(('groups', 'seq')), parts along dimension 0, may hold values from 0 to 15; in each aligned block of 64 rows (0 to 63, 64 to 127, ...) at most 8 rows name the same one
- decode_q: bfloat16 [32, 2, 8192], P(('groups', 'seq')), parts along dimension 0, may hold values from -48 to 48
- decode_k: bfloat16 [32, 2, 1024], P(('groups', 'seq')), parts along dimension 0, may hold values from -12 to 12
- decode_v: bfloat16 [32, 2, 1024], P(('groups', 'seq')), parts along dimension 0, may hold values from -4.5 to 4.5
- context_len: int32 [32], P(('groups', 'seq')), parts along dimension 0, may hold values from 768 to 6144
Outputs:
- prefill_out: bfloat16 [32, 8192], P(('groups', 'seq')), parts along dimension 0
- decode_out: bfloat16 [32, 2, 8192], P(('groups', 'seq')), parts along dimension 0
- store_k: bfloat16 [32768, 1024], P(('groups', 'seq')), parts along dimension 0
- store_v: bfloat16 [32768, 1024], P(('groups', 'seq')), parts along dimension 0
- store_page: int32 [4096], P(('groups', 'seq')), parts along dimension 0
There are 2 independent parts, one for each index of `groups`. A program takes and returns all parts, laid end to end along the dimension named above; each array names one. Nothing has to cross between parts.
Inputs may be any that keep to these rules, and one draw needn't show every extreme that they name: `page_counts`: the counts sum to 768 and the largest equals 64. `page_owner`: within the 64 page slots of one shard each owner is named at most 8 times, and exactly 8 times in some shards.
All inputs are finite; a program needn't handle non-finite values.
Results may differ from a plain program's by a relative error of at most 0.014.
Values may be sent and summed in bfloat16 or wider, within the bound.
No kernel may reach another device: no remote copies, remote signals or barrier semaphores. Data moves between devices by JAX's collectives and lax.ppermute only.
A program may use at most 128 MiB of HBM per device.

v0:
```python
import functools
import jax
import jax.numpy as jnp
from jax import lax
from jax.experimental import pallas as pl
from jax.experimental.pallas import tpu as pltpu
from jax.sharding import PartitionSpec as P

HQ = 64
KVH = 8
HD = 128
PAGE = 8
STEPS = 2
KVD = 1024
GRP = HQ // KVH
MASKED = -1e30
VMEM = pltpu.MemorySpace.VMEM
SMEM = pltpu.MemorySpace.SMEM
LIMIT = 32 * 1024 * 1024
SMALL = 8 * 1024 * 1024


def whole(space):
    return pl.BlockSpec(memory_space=space)


def message_kernel(rows_p, rows_d, length, prefill_q, decode_q, owners, out, rows):
    for r in range(rows_p + rows_d):
        ref, at = (prefill_q, r) if r < rows_p else (decode_q, r - rows_p)
        line = ref[at : at + 1, :].astype(jnp.float32)
        for h in range(HQ):
            rows[r * HQ + h : r * HQ + h + 1, :] = line[:, h * HD : (h + 1) * HD]
    base = (rows_p + rows_d) * HQ
    slots = owners.shape[1]
    rows[base : base + 8, :] = jnp.zeros((8, 128), jnp.float32)
    rows[base : base + 1, 0:slots] = owners[...].astype(jnp.float32)
    lane = lax.broadcasted_iota(jnp.int32, (1, 128), 1)
    digits = jnp.zeros((1, 128), jnp.int32)
    for q in range(length.shape[1]):
        value = length[:, q : q + 1]
        digits = jnp.where(lane == 2 * q, value >> 8, digits)
        digits = jnp.where(lane == 2 * q + 1, value & 255, digits)
    rows[base + 1 : base + 2, :] = digits.astype(jnp.float32)
    out[...] = rows[...].reshape(out.shape).astype(jnp.bfloat16)


def make_message(prefill_q, decode_q, page_owner, context_len):
    rows_p = prefill_q.shape[0]
    rows_d = decode_q.shape[0] * STEPS
    blocks = (rows_p + rows_d) * KVH + 1
    return pl.pallas_call(
        functools.partial(message_kernel, rows_p, rows_d),
        out_shape=jax.ShapeDtypeStruct((blocks, 8, 128), jnp.bfloat16),
        in_specs=[whole(VMEM)] * 4,
        out_specs=whole(VMEM),
        scratch_shapes=[pltpu.VMEM((blocks * 8, 128), jnp.float32)],
        name="message",
    )(context_len.reshape(1, -1), prefill_q, decode_q.reshape(rows_d, HQ * HD), page_owner.reshape(1, -1))


def pack_kernel(shards, capacity, partners, owners, counts, keys, values, *refs):
    outs, (taken, chosen) = refs[:-2], refs[-2:]
    me = lax.axis_index("seq")

    def reset(o, carry):
        taken[o] = 0
        return carry

    lax.fori_loop(0, shards, reset, 0, unroll=8)

    def note(j, carry):
        o = owners[j]
        k = taken[o]
        taken[o] = k + 1
        chosen[o * capacity + k] = j
        return carry

    lax.fori_loop(0, counts[me], note, 0)
    for partner, out in zip(partners, outs):
        o = me ^ partner
        count = taken[o]

        def copy(k, carry, o=o, count=count, out=out):
            full = k < count
            j = jnp.where(full, chosen[o * capacity + k], 0)
            for part, pages in enumerate((keys, values)):
                page = pages[j]
                out[part, k] = jnp.where(full, page, jnp.zeros_like(page))
            return carry

        lax.fori_loop(0, capacity, copy, 0, unroll=2)


def pack(owners, counts, keys, values, shards, capacity, partners):
    slots = keys.shape[0]
    piece = jax.ShapeDtypeStruct((2, capacity, PAGE, KVD), keys.dtype)
    return pl.pallas_call(
        functools.partial(pack_kernel, shards, capacity, partners),
        out_shape=(piece,) * len(partners),
        in_specs=[whole(SMEM), whole(SMEM), whole(VMEM), whole(VMEM)],
        out_specs=(whole(VMEM),) * len(partners),
        scratch_shapes=[
            pltpu.SMEM((shards,), jnp.int32),
            pltpu.SMEM((shards * capacity,), jnp.int32),
        ],
        cost_estimate=pl.CostEstimate(
            flops=0,
            transcendentals=0,
            bytes_accessed=(2 * slots + 4 * len(partners) * capacity) * PAGE * KVD * 2,
        ),
        name="pack",
    )(owners, counts, keys, values)


def pick_kernel(capacity, partner, owners, counts, keys, values, out, sem):
    me = lax.axis_index("seq")
    wanted = me ^ partner

    def fetch(j, k, start):
        for part, pages in enumerate((keys, values)):
            copy = pltpu.make_async_copy(pages.at[j], out.at[part, k], sem)
            if start:
                copy.start()
            else:
                copy.wait()

    def look(j, k):
        match = owners[j] == wanted

        @pl.when(match)
        def _():
            fetch(j, k, True)

        return k + match.astype(jnp.int32)

    found = lax.fori_loop(0, counts[me], look, jnp.int32(0))
    blank = jnp.zeros(out.shape[2:], out.dtype)

    def clear(k, carry):
        for part in range(2):
            out[part, k] = blank
        return carry

    lax.fori_loop(found, capacity, clear, 0)

    def arrive(k, carry):
        fetch(0, k, False)
        return carry

    lax.fori_loop(0, found, arrive, 0)


def pick(owners, counts, keys, values, capacity, partner):
    return pl.pallas_call(
        functools.partial(pick_kernel, capacity, partner),
        out_shape=jax.ShapeDtypeStruct((2, capacity, PAGE, KVD), keys.dtype),
        in_specs=[whole(SMEM), whole(SMEM), whole(pl.ANY), whole(pl.ANY)],
        out_specs=whole(VMEM),
        scratch_shapes=[pltpu.SemaphoreType.DMA],
        cost_estimate=pl.CostEstimate(
            flops=0, transcendentals=0, bytes_accessed=8 * capacity * PAGE * KVD
        ),
        name="pick",
    )(owners, counts, keys, values)


def attend_kernel(rows_p, rows_d, capacity, counts, *refs):
    messages, refs = refs[:4], refs[4:]
    keys, values, keep, give, table, limits, stats, hits = refs
    me = lax.axis_index("seq")
    rows = rows_p + rows_d
    blocks = rows * KVH + 1
    shards = 4 * messages[0].shape[0] // blocks
    height = shards * rows * GRP
    held = keys.shape[0]

    def block(k, at):
        return messages[k % 4][(k // 4) * blocks + at]

    def count(d, carry):
        before, total = carry
        here = counts[d]
        return (before + jnp.where(d < me, here, 0), total + here)

    before, total = lax.fori_loop(0, shards, count, (jnp.int32(0), jnp.int32(0)))
    start = PAGE * before
    live = PAGE * counts[me]
    first = PAGE * total - shards * rows_p + 1
    lane = lax.broadcasted_iota(jnp.int32, (1, 128), 1)
    for k in range(shards):
        d = me ^ k
        tail = block(k, rows * KVH).astype(jnp.float32)
        for r in range(rows):
            at = (k * rows + r) * GRP
            if r < rows_p:
                bound = jnp.minimum(first + d * rows_p + r - start, live)
                limits[at : at + GRP, :] = jnp.full((GRP, 128), bound, jnp.int32)
            else:
                q = (r - rows_p) // STEPS
                length = tail[1:2, 2 * q : 2 * q + 1] * 256.0 + tail[1:2, 2 * q + 1 : 2 * q + 2]
                bound = jnp.minimum(length.astype(jnp.int32) - start, live)
                limits[at : at + GRP, :] = jnp.broadcast_to(bound, (GRP, 128))
        hit = (tail[0:1, :].astype(jnp.int32) == me) & (lane < counts[d])
        hits[pl.ds(d, 1), :] = hit.astype(jnp.float32)

    hit = hits[...]
    earlier = (
        lax.broadcasted_iota(jnp.int32, (128, 128), 0)
        < lax.broadcasted_iota(jnp.int32, (128, 128), 1)
    ).astype(jnp.bfloat16)
    rank = jnp.dot(hit.astype(jnp.bfloat16), earlier, preferred_element_type=jnp.float32)
    wide = lax.broadcasted_iota(jnp.int32, hit.shape, 1)
    depth = lax.broadcasted_iota(jnp.int32, hit.shape, 0)
    numbered = jnp.zeros(hit.shape, jnp.float32)
    for k in range(capacity):
        match = jnp.where((hit > 0.5) & (rank == float(k)), (wide + 1).astype(jnp.float32), 0.0)
        found = jnp.sum(match, axis=1, keepdims=True)
        numbered = jnp.where(wide == k, found, numbered)
    within = numbered.astype(jnp.int32)
    slots = held // PAGE
    table[...] = jnp.where(within > 0, depth * slots + within - 1, -1)

    stats[...] = jnp.zeros_like(stats)
    spot = lax.broadcasted_iota(jnp.int32, (height, 128), 1)
    column = lax.broadcasted_iota(jnp.int32, (height, held), 1)
    pieces = [(k, r, (k * rows + r) * GRP) for k in range(shards) for r in range(rows)]

    def target(k):
        return give if k % 2 else keep

    def one_group(g, carry):
        query = jnp.concatenate(
            [block(k, r * KVH + g).astype(jnp.float32) for k, r, _ in pieces], axis=0
        ).astype(jnp.bfloat16)
        across = pl.ds(pl.multiple_of(g * HD, HD), HD)
        scores = lax.dot_general(
            query, keys[:, across], (((1,), (1,)), ((), ())), preferred_element_type=jnp.float32
        ) * (HD ** (-0.5))
        allowed = column < jnp.concatenate([limits[...]] * (held // 128), axis=1)
        scores = jnp.where(allowed, scores, MASKED)
        high = jnp.max(scores, axis=1, keepdims=True).astype(jnp.bfloat16).astype(jnp.float32)
        weights = jnp.where(allowed, jnp.exp(scores - high), 0.0)
        total = jnp.sum(weights, axis=1, keepdims=True)
        product = jnp.dot(
            weights.astype(jnp.bfloat16), values[:, across], preferred_element_type=jnp.float32
        )
        coarse = total.astype(jnp.bfloat16).astype(jnp.float32)
        kept = jnp.where(spot == g, high, stats[...])
        kept = jnp.where(spot == KVH + g, coarse, kept)
        stats[...] = jnp.where(spot == 2 * KVH + g, total - coarse, kept)
        for k, r, at in pieces:
            target(k)[k // 2, r * KVH + g] = product[at : at + GRP, :].astype(jnp.bfloat16)
        return carry

    lax.fori_loop(0, KVH, one_group, 0)
    for k, r, at in pieces:
        target(k)[k // 2, rows * KVH + r] = stats[at : at + GRP, :].astype(jnp.bfloat16)


def attend(rows_p, rows_d, capacity, counts, messages, keys, values):
    rows = rows_p + rows_d
    shards = 4 * messages[0].shape[0] // (rows * KVH + 1)
    height = shards * rows * GRP
    held = keys.shape[0]
    half = jax.ShapeDtypeStruct((shards // 2, rows * (KVH + 1), GRP, 128), jnp.bfloat16)
    return pl.pallas_call(
        functools.partial(attend_kernel, rows_p, rows_d, capacity),
        out_shape=(half, half, jax.ShapeDtypeStruct((shards, 128), jnp.int32)),
        in_specs=[whole(SMEM)] + [whole(VMEM)] * 6,
        out_specs=(whole(VMEM),) * 3,
        scratch_shapes=[
            pltpu.VMEM((height, 128), jnp.int32),
            pltpu.VMEM((height, 128), jnp.float32),
            pltpu.VMEM((shards, 128), jnp.float32),
        ],
        compiler_params=pltpu.CompilerParams(vmem_limit_bytes=LIMIT),
        cost_estimate=pl.CostEstimate(
            flops=4 * height * KVH * held * HD,
            transcendentals=height * KVH * held,
            bytes_accessed=2 * held * KVD * 2 + 4 * height * KVH * HD,
        ),
        name="attend",
    )(counts, *messages, keys, values)


def fold_kernel(rows, keep, got, *outs):
    lane = lax.broadcasted_iota(jnp.int32, (GRP, 128), 1)
    inside = lane < KVH

    def put(j, at, value):
        outs[j % 2][j // 2, at] = value.astype(jnp.bfloat16)

    for j in range(keep.shape[0]):
        for r in range(rows):
            raw = [ref[j, rows * KVH + r].astype(jnp.float32) for ref in (keep, got)]
            high = jnp.maximum(jnp.where(inside, raw[0], 0.0), jnp.where(inside, raw[1], 0.0))
            factors = [jnp.exp(jnp.where(inside, part, 0.0) - high) for part in raw]
            sizes = [
                pltpu.roll(part, 128 - KVH, 1) + pltpu.roll(part, 128 - 2 * KVH, 1) for part in raw
            ]
            total = jnp.where(inside, factors[0] * sizes[0] + factors[1] * sizes[1], 0.0)
            coarse = total.astype(jnp.bfloat16).astype(jnp.float32)
            line = high + pltpu.roll(coarse, KVH, 1) + pltpu.roll(total - coarse, 2 * KVH, 1)
            put(j, rows * KVH + r, line)
            for g in range(KVH):
                at = r * KVH + g
                mixed = factors[0][:, g : g + 1] * keep[j, at].astype(jnp.float32)
                mixed = mixed + factors[1][:, g : g + 1] * got[j, at].astype(jnp.float32)
                put(j, at, mixed)


def fold(rows, keep, got):
    half = jax.ShapeDtypeStruct((keep.shape[0] // 2,) + keep.shape[1:], keep.dtype)
    return pl.pallas_call(
        functools.partial(fold_kernel, rows),
        out_shape=(half, half),
        in_specs=[whole(VMEM)] * 2,
        out_specs=(whole(VMEM),) * 2,
        compiler_params=pltpu.CompilerParams(vmem_limit_bytes=LIMIT),
        cost_estimate=pl.CostEstimate(
            flops=keep.size * 4, transcendentals=0, bytes_accessed=keep.size * 6
        ),
        name="fold",
    )(keep, got)


def settle_kernel(partners, old, *refs):
    refs = refs[old:]
    pieces, (store_k, store_v, sems) = refs[: len(partners)], refs[len(partners) :]
    me = lax.axis_index("seq")
    puts = []
    for partner, piece in zip(partners, pieces):
        for part, store in enumerate((store_k, store_v)):
            puts.append(
                pltpu.make_async_copy(
                    piece.at[part], store.at[me ^ partner], sems.at[len(puts)]
                )
            )
    for put in puts:
        put.start()
    for put in puts:
        put.wait()


def settle(shards, partners, pieces, stores):
    number = len(partners)
    shape = (shards,) + pieces[0].shape[1:]
    store = jax.ShapeDtypeStruct(shape, pieces[0].dtype)
    return pl.pallas_call(
        functools.partial(settle_kernel, partners, len(stores)),
        out_shape=(store, store),
        in_specs=[whole(pl.ANY)] * len(stores) + [whole(VMEM)] * number,
        out_specs=(whole(pl.ANY),) * 2,
        input_output_aliases={i: i for i in range(len(stores))},
        scratch_shapes=[pltpu.SemaphoreType.DMA((2 * number,))],
        compiler_params=pltpu.CompilerParams(vmem_limit_bytes=SMALL),
        cost_estimate=pl.CostEstimate(
            flops=0, transcendentals=0, bytes_accessed=4 * number * pieces[0].size
        ),
        name="settle",
    )(*stores, *pieces)


def merge_kernel(rows_p, rows_d, message, new_k, new_v, *refs):
    parts, (prefill_out, decode_out, lines) = refs[:-3], refs[-3:]
    sources = len(parts)
    rows = rows_p + rows_d
    lane = lax.broadcasted_iota(jnp.int32, (GRP, 128), 1)
    for r in range(rows):
        raw = [part[0, rows * KVH + r].astype(jnp.float32) for part in parts]
        high = functools.reduce(jnp.maximum, raw)
        fresh = []
        if r >= rows_p:
            request, step = divmod(r - rows_p, STEPS)
            for t in range(step + 1):
                score = jnp.zeros((GRP, 128), jnp.float32)
                for g in range(KVH):
                    query = message[r * KVH + g].astype(jnp.float32)
                    at = request * STEPS + t
                    key = new_k[at : at + 1, g * HD : (g + 1) * HD].astype(jnp.float32)
                    column = jnp.sum(query * key, axis=1, keepdims=True) * (HD ** (-0.5))
                    score = jnp.where(lane == g, column, score)
                fresh.append((request * STEPS + t, score))
                high = jnp.maximum(high, score)
        high = jnp.where(lane < KVH, high, 0.0)
        total = jnp.zeros((GRP, 128), jnp.float32)
        factors = []
        for s in range(sources):
            factor = jnp.exp(jnp.where(lane < KVH, raw[s], 0.0) - high)
            size = pltpu.roll(raw[s], 128 - KVH, 1) + pltpu.roll(raw[s], 128 - 2 * KVH, 1)
            total = total + factor * size
            factors.append(factor)
        fresh = [(at, jnp.exp(score - high)) for at, score in fresh]
        for _, weight in fresh:
            total = total + weight
        total = jnp.where(lane < KVH, total, 1.0)
        factors = [factor / total for factor in factors]
        fresh = [
            (at, (weight / total).astype(jnp.bfloat16).astype(jnp.float32)) for at, weight in fresh
        ]
        for g in range(KVH):
            result = jnp.zeros((GRP, HD), jnp.float32)
            for s in range(sources):
                block = parts[s][0, r * KVH + g].astype(jnp.float32)
                result = result + factors[s][:, g : g + 1] * block
            for at, weight in fresh:
                value = new_v[at : at + 1, g * HD : (g + 1) * HD].astype(jnp.float32)
                result = result + weight[:, g : g + 1] * value
            for h in range(GRP):
                column = (g * GRP + h) * HD
                lines[r : r + 1, column : column + HD] = result[h : h + 1, :]
    prefill_out[...] = lines[0:rows_p, :].astype(jnp.bfloat16)
    decode_out[...] = lines[rows_p:rows, :].astype(jnp.bfloat16)


def merge(rows_p, rows_d, parts, message, new_k, new_v):
    rows = rows_p + rows_d
    return pl.pallas_call(
        functools.partial(merge_kernel, rows_p, rows_d),
        out_shape=(
            jax.ShapeDtypeStruct((rows_p, HQ * HD), jnp.bfloat16),
            jax.ShapeDtypeStruct((rows_d, HQ * HD), jnp.bfloat16),
        ),
        in_specs=[whole(VMEM)] * (3 + len(parts)),
        out_specs=(whole(VMEM), whole(VMEM)),
        scratch_shapes=[pltpu.VMEM((rows, HQ * HD), jnp.float32)],
        compiler_params=pltpu.CompilerParams(vmem_limit_bytes=LIMIT),
        cost_estimate=pl.CostEstimate(
            flops=len(parts) * parts[0].size * 4,
            transcendentals=0,
            bytes_accessed=len(parts) * parts[0].size * 2,
        ),
        name="merge",
    )(message, new_k.reshape(rows_d, KVD), new_v.reshape(rows_d, KVD), *parts)


def swap(array, distance):
    shards = lax.axis_size("seq")
    return lax.ppermute(array, "seq", [(i, i ^ distance) for i in range(shards)])


def send_order(shards):
    upper = range(shards // 2, shards)
    side = range(4, shards // 2)
    plain, plain_side = [[k for k in group if not k & 2] for group in (upper, side)]
    other, other_side = [[k for k in group if k & 2] for group in (upper, side)]
    half = len(other) // 2
    first = plain[0]
    opening = plain[1:2] + plain_side[: len(plain_side) // 2] + plain[2:3]
    second = plain_side[len(plain_side) // 2 :] + plain[3:]
    third = other[:half] + other_side
    return first, opening, second, third, [1, 2, 3], other[half:]


def bits_of(shards):
    return [1 << b for b in range(shards.bit_length() - 1)]


def per_device(
    prefill_q, cache_k, cache_v, page_counts, page_owner, decode_q, decode_k, decode_v, context_len
):
    shards = lax.axis_size("seq")
    page_slots = cache_k.shape[0] // PAGE
    capacity = max(2, 2 * page_slots // shards)
    rows_p = prefill_q.shape[0]
    rows_d = decode_q.shape[0] * STEPS
    owners = page_owner.reshape(-1)
    pages_k = cache_k.reshape(page_slots, PAGE, KVD)
    pages_v = cache_v.reshape(page_slots, PAGE, KVD)
    rows = rows_p + rows_d
    first, opening, second, third, near, last = send_order(shards)
    piece = pick(owners, page_counts, pages_k, pages_v, capacity, first)
    pieces = {first: swap(piece, first)}
    message = make_message(prefill_q, decode_q, page_owner, context_len)
    far = {0: message}
    for k in range(4, shards, 4):
        far[k] = swap(message, k)
    group = [0] + opening + second + third + near + last
    packed = pack(owners, page_counts, pages_k, pages_v, shards, capacity, group)
    for k, piece in zip(group, packed):
        pieces[k] = swap(piece, k) if k else piece
    own = jnp.concatenate([far[k] for k in range(0, shards, 4)], axis=0)
    across = swap(own, 2)
    beside = swap(own, 1)
    corner = swap(across, 1)
    keep, give, table = attend(
        rows_p,
        rows_d,
        capacity,
        page_counts,
        (own, beside, across, corner),
        cache_k,
        cache_v,
    )
    for bit in bits_of(shards):
        got = swap(give, bit)
        if 2 * bit < shards:
            keep, give = fold(rows, keep, got)
    parts = (keep, got)
    prefill_out, decode_out = merge(rows_p, rows_d, parts, message, decode_k, decode_v)
    stores = ()
    for group in ([0, first] + opening + second + near, third, last):
        stores = settle(shards, group, [pieces[k] for k in group], stores)
    store_page = table[:, :capacity].reshape(-1)
    return (
        prefill_out,
        decode_out.reshape(decode_q.shape),
        stores[0].reshape(-1, KVD),
        stores[1].reshape(-1, KVD),
        store_page,
    )


def solution(mesh):
    in_specs = (
        P(("groups", "seq"), None),
        P(("groups", "seq"), None),
        P(("groups", "seq"), None),
        P("groups"),
        P(("groups", "seq"), None),
        P(("groups", "seq"), None, None),
        P(("groups", "seq"), None, None),
        P(("groups", "seq"), None, None),
        P(("groups", "seq")),
    )
    out_specs = (
        P(("groups", "seq"), None),
        P(("groups", "seq"), None, None),
        P(("groups", "seq"), None),
        P(("groups", "seq"), None),
        P(("groups", "seq")),
    )
    return jax.shard_map(
        per_device, mesh=mesh, in_specs=in_specs, out_specs=out_specs, check_vma=False
    )
```

profile of v0, /device:TPU:13, one launch (start us, length us, event | category | flops | bytes accessed | tf_op | source)
XLA Modules:
  0.0 135.0 jit_solution(867051614257939537)
XLA Ops:
  1.3 1.5 %message.1 = bf16[25,8,128]{2,1,0:T(8,128)(2,1)} custom-call(s32[1,1]{1,0:T(1,128)} %bitcast.12.length, bf16[1,8192]{1,0:T(2,128)(2,1)} %prefill_q.1, bf16[2,8192]{1,0:T(2,128)(2,1)} %bitcast.22, s32[1,64]{1,0:T(1,128)} %bitcast.23), custom_call_target="tpu_custom_call" | custom-call | tf_op jit(solution)/shard_map/message/pallas_call | solution.py:51
  2.8 0.2 collective-permute-start
  2.9 2.3 %collective-permute-start.1 = (bf16[25,8,128]{2,1,0:T(8,128)(2,1)}, bf16[25,8,128]{2,1,0:T(8,128)(2,1)S(1)}, u32[]{:S(2)}, u32[]{:S(2)}) collective-permute-start(bf16[25,8,128]{2,1,0:T(8,128)(2,1)} %message.1), channel_id=1, source_target_pairs={{0,8},{1,9},{2,10},{3,11},{4,12},{5,13},{6,14},{7,15},{8,0},{9,1},... | collective-permute-start | bytes 153608 | tf_op jit(solution)/shard_map/ppermute | solution.py:439
  5.2 0.2 collective-permute-start.2
  5.4 0.5 collective-permute-done
  5.9 1.7 %collective-permute-done.1 = bf16[25,8,128]{2,1,0:T(8,128)(2,1)S(1)} collective-permute-done((bf16[25,8,128]{2,1,0:T(8,128)(2,1)}, bf16[25,8,128]{2,1,0:T(8,128)(2,1)S(1)}, u32[]{:S(2)}, u32[]{:S(2)}) %collective-permute-start.1) | collective-permute-done | bytes 51232 | tf_op jit(solution)/shard_map/ppermute | solution.py:439
  7.6 1.8 %collective-permute-done.2 = bf16[25,8,128]{2,1,0:T(8,128)(2,1)S(1)} collective-permute-done((bf16[25,8,128]{2,1,0:T(8,128)(2,1)}, bf16[25,8,128]{2,1,0:T(8,128)(2,1)S(1)}, u32[]{:S(2)}, u32[]{:S(2)}) %collective-permute-start.2) | collective-permute-done | bytes 51232 | tf_op jit(solution)/shard_map/ppermute | solution.py:439
  9.4 0.8 pad_maximum_fusion.refs_0_
  10.2 0.3 collective-permute-start.4
  10.5 2.2 %collective-permute-start.3 = (bf16[100,8,128]{2,1,0:T(8,128)(2,1)S(1)}, bf16[100,8,128]{2,1,0:T(8,128)(2,1)S(1)}, u32[]{:S(2)}, u32[]{:S(2)}) collective-permute-start(bf16[100,8,128]{2,1,0:T(8,128)(2,1)S(1)} %pad_maximum_fusion.refs_0_), channel_id=1, source_target_pairs={{0,1},{1,0},{2,3},{3,2},{4,5},{5,4},{6,7},{7,6},{8,9},{9,8},{10,11... | collective-permute-start | bytes 614408 | tf_op jit(solution)/shard_map/ppermute | solution.py:439
  12.8 2.1 %collective-permute-done.4.refs_2_ = bf16[100,8,128]{2,1,0:T(8,128)(2,1)S(1)} collective-permute-done((bf16[100,8,128]{2,1,0:T(8,128)(2,1)S(1)}, bf16[100,8,128]{2,1,0:T(8,128)(2,1)S(1)}, u32[]{:S(2)}, u32[]{:S(2)}) %collective-permute-start.4) | collective-permute-done | bytes 204832 | tf_op jit(solution)/shard_map/ppermute | solution.py:439
  14.9 3.1 %collective-permute-start.5 = (bf16[100,8,128]{2,1,0:T(8,128)(2,1)S(1)}, bf16[100,8,128]{2,1,0:T(8,128)(2,1)S(1)}, u32[]{:S(2)}, u32[]{:S(2)}) collective-permute-start(bf16[100,8,128]{2,1,0:T(8,128)(2,1)S(1)} %collective-permute-done.4.refs_2_), channel_id=1, source_target_pairs={{0,1},{1,0},{2,3},{3,2},{4,5},{5,4},{6,7},{7,6},{8,9},{9,8},{10,11... | collective-permute-start | bytes 614408 | tf_op jit(solution)/shard_map/ppermute | solution.py:439
  18.0 0.0 collective-permute-done.3.refs_1_
  18.0 1.1 collective-permute-done.5.refs_3_
  19.1 1.2 copy-done
  20.3 1.2 copy-done.1
  21.5 0.7 copy-done.6
  22.2 7.5 %attend.1 = (bf16[8,27,8,128]{3,2,1,0:T(8,128)(2,1)S(1)}, bf16[8,27,8,128]{3,2,1,0:T(8,128)(2,1)S(1)}, s32[16,128]{1,0:T(8,128)S(1)}) custom-call(s32[16]{0:T(128)S(1)} %copy-done.6, bf16[100,8,128]{2,1,0:T(8,128)(2,1)S(1)} %pad_maximum_fusion.refs_0_, bf16[100,8,128]{2,1,0:T(8,128)(2,1)S(1)} %collective-permute-done.3.refs_1_, ...), custom_call_target="tpu_custom_call" | custom-call | flops 805306368 | bytes 3670016 | tf_op jit(solution)/shard_map/attend/pallas_call | solution.py:266
  29.7 0.4 collective-permute-start.6
  30.1 5.2 %pack.1 = (bf16[2,8,8,1024]{3,2,1,0:T(8,128)(2,1)}, bf16[2,8,8,1024]{3,2,1,0:T(8,128)(2,1)}, bf16[2,8,8,1024]{3,2,1,0:T(8,128)(2,1)}, bf16[2,8,8,1024]{3,2,1,0:T...) custom-call(s32[64]{0:T(128)} %bitcast.24, ...), custom_call_target="tpu_custom_call" | custom-call | bytes 9961472 | tf_op jit(solution)/shard_map/pack/pallas_call | solution.py:97
  35.3 2.0 %collective-permute-start.11 = (bf16[2,8,8,1024]{3,2,1,0:T(8,128)(2,1)}, bf16[2,8,8,1024]{3,2,1,0:T(8,128)(2,1)S(1)}, u32[]{:S(2)}, u32[]{:S(2)}) collective-permute-start(bf16[2,8,8,1024]{3,2,1,0:T(8,128)(2,1)} %get-tuple-element.48), channel_id=1, source_target_pairs={{0,9},{1,8},{2,11},{3,10},{4,13},{5,12},{6,15},{7,14},{8,1},{9,0},... | collective-permute-start | bytes 786440 | tf_op jit(solution)/shard_map/ppermute | solution.py:439
  37.4 0.6 collective-permute-start.12
  38.0 0.8 collective-permute-start.13
  38.8 3.5 %collective-permute-start.14 = (bf16[2,8,8,1024]{3,2,1,0:T(8,128)(2,1)}, bf16[2,8,8,1024]{3,2,1,0:T(8,128)(2,1)S(1)}, u32[]{:S(2)}, u32[]{:S(2)}) collective-permute-start(bf16[2,8,8,1024]{3,2,1,0:T(8,128)(2,1)} %get-tuple-element.51), channel_id=1, source_target_pairs={{0,5},{1,4},{2,7},{3,6},{4,1},{5,0},{6,3},{7,2},{8,13},{9,12},{10,... | collective-permute-start | bytes 786440 | tf_op jit(solution)/shard_map/ppermute | solution.py:439
  42.3 0.0 collective-permute-done.6.got
  42.3 0.0 collective-permute-start.15
  42.3 2.6 %fold.3 = (bf16[4,27,8,128]{3,2,1,0:T(8,128)(2,1)S(1)}, bf16[4,27,8,128]{3,2,1,0:T(8,128)(2,1)S(1)}) custom-call(bf16[8,27,8,128]{3,2,1,0:T(8,128)(2,1)S(1)} %get-tuple-element.37.keep, bf16[8,27,8,128]{3,2,1,0:T(8,128)(2,1)S(1)} %collective-permute-done.6.got), custom_call_target="tpu_custom_call" | custom-call | flops 884736 | bytes 1327104 | tf_op jit(solution)/shard_map/fold/pallas_call | solution.py:314
  44.9 4.5 %collective-permute-done.11.refs_2_ = bf16[2,8,8,1024]{3,2,1,0:T(8,128)(2,1)S(1)} collective-permute-done((bf16[2,8,8,1024]{3,2,1,0:T(8,128)(2,1)}, bf16[2,8,8,1024]{3,2,1,0:T(8,128)(2,1)S(1)}, u32[]{:S(2)}, u32[]{:S(2)}) %collective-permute-start.11) | collective-permute-done | bytes 262176 | tf_op jit(solution)/shard_map/ppermute | solution.py:439
  49.4 0.0 collective-permute-start.7
  49.4 0.5 collective-permute-done.12.refs_3_
  49.9 7.2 %collective-permute-start.16 = (bf16[2,8,8,1024]{3,2,1,0:T(8,128)(2,1)}, bf16[2,8,8,1024]{3,2,1,0:T(8,128)(2,1)S(1)}, u32[]{:S(2)}, u32[]{:S(2)}) collective-permute-start(bf16[2,8,8,1024]{3,2,1,0:T(8,128)(2,1)} %get-tuple-element.53), channel_id=1, source_target_pairs={{0,1},{1,0},{2,3},{3,2},{4,5},{5,4},{6,7},{7,6},{8,9},{9,8},{10,11... | collective-permute-start | bytes 786440 | tf_op jit(solution)/shard_map/ppermute | solution.py:439
  57.0 5.0 %collective-permute-done.13.refs_4_ = bf16[2,8,8,1024]{3,2,1,0:T(8,128)(2,1)S(1)} collective-permute-done((bf16[2,8,8,1024]{3,2,1,0:T(8,128)(2,1)}, bf16[2,8,8,1024]{3,2,1,0:T(8,128)(2,1)S(1)}, u32[]{:S(2)}, u32[]{:S(2)}) %collective-permute-start.13) | collective-permute-done | bytes 262176 | tf_op jit(solution)/shard_map/ppermute | solution.py:439
  62.1 0.7 collective-permute-done.14.refs_5_
  62.7 4.8 %collective-permute-start.18 = (bf16[2,8,8,1024]{3,2,1,0:T(8,128)(2,1)}, bf16[2,8,8,1024]{3,2,1,0:T(8,128)(2,1)S(1)}, u32[]{:S(2)}, u32[]{:S(2)}) collective-permute-start(bf16[2,8,8,1024]{3,2,1,0:T(8,128)(2,1)} %get-tuple-element.55), channel_id=1, source_target_pairs={{0,3},{1,2},{2,1},{3,0},{4,7},{5,6},{6,5},{7,4},{8,11},{9,10},{10,... | collective-permute-start | bytes 786440 | tf_op jit(solution)/shard_map/ppermute | solution.py:439
  67.6 2.6 %pick.1 = bf16[2,8,8,1024]{3,2,1,0:T(8,128)(2,1)} custom-call(s32[64]{0:T(128)} %bitcast.25, s32[16]{0:T(128)} %counts.5, bf16[64,8,1024]{2,1,0:T(8,128)(2,1)} %bitcast.14, bf16[64,8,1024]{2,1,0:T(8,128)(2,1)} %bitcast.16), custom_call_target="tpu_custom_call" | custom-call | bytes 524288 | tf_op jit(solution)/shard_map/pick/pallas_call | solution.py:154
  70.1 2.8 %collective-permute-done.15.refs_6_ = bf16[2,8,8,1024]{3,2,1,0:T(8,128)(2,1)S(1)} collective-permute-done((bf16[2,8,8,1024]{3,2,1,0:T(8,128)(2,1)}, bf16[2,8,8,1024]{3,2,1,0:T(8,128)(2,1)S(1)}, u32[]{:S(2)}, u32[]{:S(2)}) %collective-permute-start.15) | collective-permute-done | bytes 262176 | tf_op jit(solution)/shard_map/ppermute | solution.py:439
  73.0 0.0 collective-permute-start.10
  73.0 0.0 collective-permute-done.7.got
  73.0 2.0 %collective-permute-start.19 = (bf16[2,8,8,1024]{3,2,1,0:T(8,128)(2,1)}, bf16[2,8,8,1024]{3,2,1,0:T(8,128)(2,1)S(1)}, u32[]{:S(2)}, u32[]{:S(2)}) collective-permute-start(bf16[2,8,8,1024]{3,2,1,0:T(8,128)(2,1)} %get-tuple-element.58), channel_id=1, source_target_pairs={{0,10},{1,11},{2,8},{3,9},{4,14},{5,15},{6,12},{7,13},{8,2},{9,3},... | collective-permute-start | bytes 786440 | tf_op jit(solution)/shard_map/ppermute | solution.py:439
  75.0 1.2 fold.4
  76.1 0.0 collective-permute-done.16.refs_7_
  76.1 0.3 collective-permute-start.8
  76.5 0.0 collective-permute-done.17.refs_8_
  76.5 4.3 %collective-permute-start.20 = (bf16[2,8,8,1024]{3,2,1,0:T(8,128)(2,1)}, bf16[2,8,8,1024]{3,2,1,0:T(8,128)(2,1)S(1)}, u32[]{:S(2)}, u32[]{:S(2)}) collective-permute-start(bf16[2,8,8,1024]{3,2,1,0:T(8,128)(2,1)} %get-tuple-element.59), channel_id=1, source_target_pairs={{0,11},{1,10},{2,9},{3,8},{4,15},{5,14},{6,13},{7,12},{8,3},{9,2},... | collective-permute-start | bytes 786440 | tf_op jit(solution)/shard_map/ppermute | solution.py:439
  80.8 0.0 collective-permute-done.18.refs_9_
  80.8 0.0 collective-permute-start.21
  80.8 14.4 %collective-permute-done.10.refs_1_ = bf16[2,8,8,1024]{3,2,1,0:T(8,128)(2,1)S(1)} collective-permute-done((bf16[2,8,8,1024]{3,2,1,0:T(8,128)(2,1)}, bf16[2,8,8,1024]{3,2,1,0:T(8,128)(2,1)S(1)}, u32[]{:S(2)}, u32[]{:S(2)}) %collective-permute-start.10) | collective-permute-done | bytes 262176 | tf_op jit(solution)/shard_map/ppermute | solution.py:439
  95.2 4.7 %collective-permute-start.22 = (bf16[2,8,8,1024]{3,2,1,0:T(8,128)(2,1)}, bf16[2,8,8,1024]{3,2,1,0:T(8,128)(2,1)S(1)}, u32[]{:S(2)}, u32[]{:S(2)}) collective-permute-start(bf16[2,8,8,1024]{3,2,1,0:T(8,128)(2,1)} %get-tuple-element.61), channel_id=1, source_target_pairs={{0,7},{1,6},{2,5},{3,4},{4,3},{5,2},{6,1},{7,0},{8,15},{9,14},{10,... | collective-permute-start | bytes 786440 | tf_op jit(solution)/shard_map/ppermute | solution.py:439
  99.9 1.6 %collective-permute-done.19.refs_2_ = bf16[2,8,8,1024]{3,2,1,0:T(8,128)(2,1)S(1)} collective-permute-done((bf16[2,8,8,1024]{3,2,1,0:T(8,128)(2,1)}, bf16[2,8,8,1024]{3,2,1,0:T(8,128)(2,1)S(1)}, u32[]{:S(2)}, u32[]{:S(2)}) %collective-permute-start.19) | collective-permute-done | bytes 262176 | tf_op jit(solution)/shard_map/ppermute | solution.py:439
  101.4 0.0 collective-permute-start.23
  101.4 0.0 collective-permute-done.8.got
  101.5 3.9 %collective-permute-start.24 = (bf16[2,8,8,1024]{3,2,1,0:T(8,128)(2,1)S(1)}, bf16[2,8,8,1024]{3,2,1,0:T(8,128)(2,1)S(1)}, u32[]{:S(2)}, u32[]{:S(2)}) collective-permute-start(bf16[2,8,8,1024]{3,2,1,0:T(8,128)(2,1)S(1)} %copy-done.7), channel_id=1, source_target_pairs={{0,15},{1,14},{2,13},{3,12},{4,11},{5,10},{6,9},{7,8},{8,7},{9,6},... | collective-permute-start | bytes 786440 | tf_op jit(solution)/shard_map/ppermute | solution.py:439
  105.3 0.5 fold.5
  105.8 1.2 collective-permute-done.20.refs_3_
  107.1 14.6 %collective-permute-start.9 = (bf16[1,27,8,128]{3,2,1,0:T(8,128)(2,1)S(1)}, bf16[1,27,8,128]{3,2,1,0:T(8,128)(2,1)S(1)}, u32[]{:S(2)}, u32[]{:S(2)}) collective-permute-start(bf16[1,27,8,128]{3,2,1,0:T(8,128)(2,1)S(1)} %get-tuple-element.44), channel_id=1, source_target_pairs={{0,8},{1,9},{2,10},{3,11},{4,12},{5,13},{6,14},{7,15},{8,0},{9,1},... | collective-permute-start | bytes 165896 | tf_op jit(solution)/shard_map/ppermute | solution.py:439
  121.6 1.6 %settle.3 = (bf16[16,8,8,1024]{3,2,1,0:T(8,128)(2,1)}, bf16[16,8,8,1024]{3,2,1,0:T(8,128)(2,1)}) custom-call(bf16[2,8,8,1024]{3,2,1,0:T(8,128)(2,1)S(1)} %copy-done.3, bf16[2,8,8,1024]{3,2,1,0:T(8,128)(2,1)S(1)} %collective-permute-done.10.refs_1_, bf16[2,8,8,1024]{3,2,1,0:T(8,128)(2,1)S(1)} %collective-permute-done.11.refs_2_, ...), custom_call_target="tpu_custom_call" | custom-call | bytes 5242880 | tf_op jit(solution)/shard_map/settle/pallas_call | solution.py:349
  123.3 0.0 collective-permute-done.21.refs_4_
  123.3 1.8 %collective-permute-done.22.refs_5_ = bf16[2,8,8,1024]{3,2,1,0:T(8,128)(2,1)S(1)} collective-permute-done((bf16[2,8,8,1024]{3,2,1,0:T(8,128)(2,1)}, bf16[2,8,8,1024]{3,2,1,0:T(8,128)(2,1)S(1)}, u32[]{:S(2)}, u32[]{:S(2)}) %collective-permute-start.22) | collective-permute-done | bytes 262176 | tf_op jit(solution)/shard_map/ppermute | solution.py:439
  125.1 1.0 settle.4
  126.2 6.3 %collective-permute-done.24.refs_3_ = bf16[2,8,8,1024]{3,2,1,0:T(8,128)(2,1)S(1)} collective-permute-done((bf16[2,8,8,1024]{3,2,1,0:T(8,128)(2,1)S(1)}, bf16[2,8,8,1024]{3,2,1,0:T(8,128)(2,1)S(1)}, u32[]{:S(2)}, u32[]{:S(2)}) %collective-permute-start.24) | collective-permute-done | bytes 262176 | tf_op jit(solution)/shard_map/ppermute | solution.py:439
  132.5 0.8 settle.5
  133.3 0.6 reshape.57
  133.9 0.0 collective-permute-done.9.refs_1_
  133.9 1.1 merge.1
  (15 shorter events, 0.0 us)
Async XLA Ops:
  2.8 3.2 %collective-permute-start = (bf16[25,8,128]{2,1,0:T(8,128)(2,1)}, bf16[25,8,128]{2,1,0:T(8,128)(2,1)S(1)}, u32[]{:S(2)}, u32[]{:S(2)}) collective-permute-start(bf16[25,8,128]{2,1,0:T(8,128)(2,1)} %message.1), channel_id=1, source_target_pairs={{0,4},{1,5},{2,6},{3,7},{4,0},{5,1},{6,2},{7,3},{8,12},{9,13},{10,... | collective-permute-start | bytes 153608 | tf_op jit(solution)/shard_map/ppermute | solution.py:439
  2.9 4.7 %collective-permute-start.1 = (bf16[25,8,128]{2,1,0:T(8,128)(2,1)}, bf16[25,8,128]{2,1,0:T(8,128)(2,1)S(1)}, u32[]{:S(2)}, u32[]{:S(2)}) collective-permute-start(bf16[25,8,128]{2,1,0:T(8,128)(2,1)} %message.1), channel_id=1, source_target_pairs={{0,8},{1,9},{2,10},{3,11},{4,12},{5,13},{6,14},{7,15},{8,0},{9,1},... | collective-permute-start | bytes 153608 | tf_op jit(solution)/shard_map/ppermute | solution.py:439
  5.2 4.1 %collective-permute-start.2 = (bf16[25,8,128]{2,1,0:T(8,128)(2,1)}, bf16[25,8,128]{2,1,0:T(8,128)(2,1)S(1)}, u32[]{:S(2)}, u32[]{:S(2)}) collective-permute-start(bf16[25,8,128]{2,1,0:T(8,128)(2,1)} %message.1), channel_id=1, source_target_pairs={{0,12},{1,13},{2,14},{3,15},{4,8},{5,9},{6,10},{7,11},{8,4},{9,5},... | collective-permute-start | bytes 153608 | tf_op jit(solution)/shard_map/ppermute | solution.py:439
  10.2 4.7 %collective-permute-start.4 = (bf16[100,8,128]{2,1,0:T(8,128)(2,1)S(1)}, bf16[100,8,128]{2,1,0:T(8,128)(2,1)S(1)}, u32[]{:S(2)}, u32[]{:S(2)}) collective-permute-start(bf16[100,8,128]{2,1,0:T(8,128)(2,1)S(1)} %pad_maximum_fusion.refs_0_), channel_id=1, source_target_pairs={{0,2},{1,3},{2,0},{3,1},{4,6},{5,7},{6,4},{7,5},{8,10},{9,11},{10,... | collective-permute-start | bytes 614408 | tf_op jit(solution)/shard_map/ppermute | solution.py:439
  10.5 7.5 %collective-permute-start.3 = (bf16[100,8,128]{2,1,0:T(8,128)(2,1)S(1)}, bf16[100,8,128]{2,1,0:T(8,128)(2,1)S(1)}, u32[]{:S(2)}, u32[]{:S(2)}) collective-permute-start(bf16[100,8,128]{2,1,0:T(8,128)(2,1)S(1)} %pad_maximum_fusion.refs_0_), channel_id=1, source_target_pairs={{0,1},{1,0},{2,3},{3,2},{4,5},{5,4},{6,7},{7,6},{8,9},{9,8},{10,11... | collective-permute-start | bytes 614408 | tf_op jit(solution)/shard_map/ppermute | solution.py:439
  14.9 4.2 %collective-permute-start.5 = (bf16[100,8,128]{2,1,0:T(8,128)(2,1)S(1)}, bf16[100,8,128]{2,1,0:T(8,128)(2,1)S(1)}, u32[]{:S(2)}, u32[]{:S(2)}) collective-permute-start(bf16[100,8,128]{2,1,0:T(8,128)(2,1)S(1)} %collective-permute-done.4.refs_2_), channel_id=1, source_target_pairs={{0,1},{1,0},{2,3},{3,2},{4,5},{5,4},{6,7},{7,6},{8,9},{9,8},{10,11... | collective-permute-start | bytes 614408 | tf_op jit(solution)/shard_map/ppermute | solution.py:439
  19.1 1.2 copy-start
  20.3 1.2 copy-start.1
  21.5 0.7 copy-start.6
  29.7 12.6 %collective-permute-start.6 = (bf16[8,27,8,128]{3,2,1,0:T(8,128)(2,1)S(1)}, bf16[8,27,8,128]{3,2,1,0:T(8,128)(2,1)S(1)}, u32[]{:S(2)}, u32[]{:S(2)}) collective-permute-start(bf16[8,27,8,128]{3,2,1,0:T(8,128)(2,1)S(1)} %get-tuple-element.38), channel_id=1, source_target_pairs={{0,1},{1,0},{2,3},{3,2},{4,5},{5,4},{6,7},{7,6},{8,9},{9,8},{10,11... | collective-permute-start | bytes 1327112 | tf_op jit(solution)/shard_map/ppermute | solution.py:439
  35.3 66.1 %copy-start.7 = (bf16[2,8,8,1024]{3,2,1,0:T(8,128)(2,1)S(1)}, bf16[2,8,8,1024]{3,2,1,0:T(8,128)(2,1)}, u32[]{:S(2)}) copy-start(bf16[2,8,8,1024]{3,2,1,0:T(8,128)(2,1)} %get-tuple-element.65) | copy-start | bytes 786436
  35.3 86.3 %copy-start.3 = (bf16[2,8,8,1024]{3,2,1,0:T(8,128)(2,1)S(1)}, bf16[2,8,8,1024]{3,2,1,0:T(8,128)(2,1)}, u32[]{:S(2)}) copy-start(bf16[2,8,8,1024]{3,2,1,0:T(8,128)(2,1)} %get-tuple-element.47.refs_0_) | copy-start | bytes 786436
  35.3 14.1 %collective-permute-start.11 = (bf16[2,8,8,1024]{3,2,1,0:T(8,128)(2,1)}, bf16[2,8,8,1024]{3,2,1,0:T(8,128)(2,1)S(1)}, u32[]{:S(2)}, u32[]{:S(2)}) collective-permute-start(bf16[2,8,8,1024]{3,2,1,0:T(8,128)(2,1)} %get-tuple-element.48), channel_id=1, source_target_pairs={{0,9},{1,8},{2,11},{3,10},{4,13},{5,12},{6,15},{7,14},{8,1},{9,0},... | collective-permute-start | bytes 786440 | tf_op jit(solution)/shard_map/ppermute | solution.py:439
  37.4 12.5 %collective-permute-start.12 = (bf16[2,8,8,1024]{3,2,1,0:T(8,128)(2,1)}, bf16[2,8,8,1024]{3,2,1,0:T(8,128)(2,1)S(1)}, u32[]{:S(2)}, u32[]{:S(2)}) collective-permute-start(bf16[2,8,8,1024]{3,2,1,0:T(8,128)(2,1)} %get-tuple-element.49), channel_id=1, source_target_pairs={{0,4},{1,5},{2,6},{3,7},{4,0},{5,1},{6,2},{7,3},{8,12},{9,13},{10,... | collective-permute-start | bytes 786440 | tf_op jit(solution)/shard_map/ppermute | solution.py:439
  38.0 24.1 %collective-permute-start.13 = (bf16[2,8,8,1024]{3,2,1,0:T(8,128)(2,1)}, bf16[2,8,8,1024]{3,2,1,0:T(8,128)(2,1)S(1)}, u32[]{:S(2)}, u32[]{:S(2)}) collective-permute-start(bf16[2,8,8,1024]{3,2,1,0:T(8,128)(2,1)} %get-tuple-element.50), channel_id=1, source_target_pairs={{0,12},{1,13},{2,14},{3,15},{4,8},{5,9},{6,10},{7,11},{8,4},{9,5},... | collective-permute-start | bytes 786440 | tf_op jit(solution)/shard_map/ppermute | solution.py:439
  38.8 23.9 %collective-permute-start.14 = (bf16[2,8,8,1024]{3,2,1,0:T(8,128)(2,1)}, bf16[2,8,8,1024]{3,2,1,0:T(8,128)(2,1)S(1)}, u32[]{:S(2)}, u32[]{:S(2)}) collective-permute-start(bf16[2,8,8,1024]{3,2,1,0:T(8,128)(2,1)} %get-tuple-element.51), channel_id=1, source_target_pairs={{0,5},{1,4},{2,7},{3,6},{4,1},{5,0},{6,3},{7,2},{8,13},{9,12},{10,... | collective-permute-start | bytes 786440 | tf_op jit(solution)/shard_map/ppermute | solution.py:439
  42.3 30.7 %collective-permute-start.15 = (bf16[2,8,8,1024]{3,2,1,0:T(8,128)(2,1)}, bf16[2,8,8,1024]{3,2,1,0:T(8,128)(2,1)S(1)}, u32[]{:S(2)}, u32[]{:S(2)}) collective-permute-start(bf16[2,8,8,1024]{3,2,1,0:T(8,128)(2,1)} %get-tuple-element.52), channel_id=1, source_target_pairs={{0,13},{1,12},{2,15},{3,14},{4,9},{5,8},{6,11},{7,10},{8,5},{9,4},... | collective-permute-start | bytes 786440 | tf_op jit(solution)/shard_map/ppermute | solution.py:439
  49.4 23.6 %collective-permute-start.7 = (bf16[4,27,8,128]{3,2,1,0:T(8,128)(2,1)S(1)}, bf16[4,27,8,128]{3,2,1,0:T(8,128)(2,1)S(1)}, u32[]{:S(2)}, u32[]{:S(2)}) collective-permute-start(bf16[4,27,8,128]{3,2,1,0:T(8,128)(2,1)S(1)} %get-tuple-element.40), channel_id=1, source_target_pairs={{0,2},{1,3},{2,0},{3,1},{4,6},{5,7},{6,4},{7,5},{8,10},{9,11},{10,... | collective-permute-start | bytes 663560 | tf_op jit(solution)/shard_map/ppermute | solution.py:439
  49.9 26.3 %collective-permute-start.16 = (bf16[2,8,8,1024]{3,2,1,0:T(8,128)(2,1)}, bf16[2,8,8,1024]{3,2,1,0:T(8,128)(2,1)S(1)}, u32[]{:S(2)}, u32[]{:S(2)}) collective-permute-start(bf16[2,8,8,1024]{3,2,1,0:T(8,128)(2,1)} %get-tuple-element.53), channel_id=1, source_target_pairs={{0,1},{1,0},{2,3},{3,2},{4,5},{5,4},{6,7},{7,6},{8,9},{9,8},{10,11... | collective-permute-start | bytes 786440 | tf_op jit(solution)/shard_map/ppermute | solution.py:439
  62.1 14.4 %collective-permute-start.17 = (bf16[2,8,8,1024]{3,2,1,0:T(8,128)(2,1)}, bf16[2,8,8,1024]{3,2,1,0:T(8,128)(2,1)S(1)}, u32[]{:S(2)}, u32[]{:S(2)}) collective-permute-start(bf16[2,8,8,1024]{3,2,1,0:T(8,128)(2,1)} %get-tuple-element.54), channel_id=1, source_target_pairs={{0,2},{1,3},{2,0},{3,1},{4,6},{5,7},{6,4},{7,5},{8,10},{9,11},{10,... | collective-permute-start | bytes 786440 | tf_op jit(solution)/shard_map/ppermute | solution.py:439
  62.7 18.1 %collective-permute-start.18 = (bf16[2,8,8,1024]{3,2,1,0:T(8,128)(2,1)}, bf16[2,8,8,1024]{3,2,1,0:T(8,128)(2,1)S(1)}, u32[]{:S(2)}, u32[]{:S(2)}) collective-permute-start(bf16[2,8,8,1024]{3,2,1,0:T(8,128)(2,1)} %get-tuple-element.55), channel_id=1, source_target_pairs={{0,3},{1,2},{2,1},{3,0},{4,7},{5,6},{6,5},{7,4},{8,11},{9,10},{10,... | collective-permute-start | bytes 786440 | tf_op jit(solution)/shard_map/ppermute | solution.py:439
  73.0 22.2 %collective-permute-start.10 = (bf16[2,8,8,1024]{3,2,1,0:T(8,128)(2,1)}, bf16[2,8,8,1024]{3,2,1,0:T(8,128)(2,1)S(1)}, u32[]{:S(2)}, u32[]{:S(2)}) collective-permute-start(bf16[2,8,8,1024]{3,2,1,0:T(8,128)(2,1)} %pick.1), channel_id=1, source_target_pairs={{0,8},{1,9},{2,10},{3,11},{4,12},{5,13},{6,14},{7,15},{8,0},{9,1},... | collective-permute-start | bytes 786440 | tf_op jit(solution)/shard_map/ppermute | solution.py:439
  73.0 28.5 %collective-permute-start.19 = (bf16[2,8,8,1024]{3,2,1,0:T(8,128)(2,1)}, bf16[2,8,8,1024]{3,2,1,0:T(8,128)(2,1)S(1)}, u32[]{:S(2)}, u32[]{:S(2)}) collective-permute-start(bf16[2,8,8,1024]{3,2,1,0:T(8,128)(2,1)} %get-tuple-element.58), channel_id=1, source_target_pairs={{0,10},{1,11},{2,8},{3,9},{4,14},{5,15},{6,12},{7,13},{8,2},{9,3},... | collective-permute-start | bytes 786440 | tf_op jit(solution)/shard_map/ppermute | solution.py:439
  76.1 25.3 %collective-permute-start.8 = (bf16[2,27,8,128]{3,2,1,0:T(8,128)(2,1)S(1)}, bf16[2,27,8,128]{3,2,1,0:T(8,128)(2,1)S(1)}, u32[]{:S(2)}, u32[]{:S(2)}) collective-permute-start(bf16[2,27,8,128]{3,2,1,0:T(8,128)(2,1)S(1)} %get-tuple-element.42), channel_id=1, source_target_pairs={{0,4},{1,5},{2,6},{3,7},{4,0},{5,1},{6,2},{7,3},{8,12},{9,13},{10,... | collective-permute-start | bytes 331784 | tf_op jit(solution)/shard_map/ppermute | solution.py:439
  76.5 30.6 %collective-permute-start.20 = (bf16[2,8,8,1024]{3,2,1,0:T(8,128)(2,1)}, bf16[2,8,8,1024]{3,2,1,0:T(8,128)(2,1)S(1)}, u32[]{:S(2)}, u32[]{:S(2)}) collective-permute-start(bf16[2,8,8,1024]{3,2,1,0:T(8,128)(2,1)} %get-tuple-element.59), channel_id=1, source_target_pairs={{0,11},{1,10},{2,9},{3,8},{4,15},{5,14},{6,13},{7,12},{8,3},{9,2},... | collective-permute-start | bytes 786440 | tf_op jit(solution)/shard_map/ppermute | solution.py:439
  80.8 42.5 %collective-permute-start.21 = (bf16[2,8,8,1024]{3,2,1,0:T(8,128)(2,1)}, bf16[2,8,8,1024]{3,2,1,0:T(8,128)(2,1)S(1)}, u32[]{:S(2)}, u32[]{:S(2)}) collective-permute-start(bf16[2,8,8,1024]{3,2,1,0:T(8,128)(2,1)} %get-tuple-element.60), channel_id=1, source_target_pairs={{0,6},{1,7},{2,4},{3,5},{4,2},{5,3},{6,0},{7,1},{8,14},{9,15},{10,... | collective-permute-start | bytes 786440 | tf_op jit(solution)/shard_map/ppermute | solution.py:439
  95.2 30.0 %collective-permute-start.22 = (bf16[2,8,8,1024]{3,2,1,0:T(8,128)(2,1)}, bf16[2,8,8,1024]{3,2,1,0:T(8,128)(2,1)S(1)}, u32[]{:S(2)}, u32[]{:S(2)}) collective-permute-start(bf16[2,8,8,1024]{3,2,1,0:T(8,128)(2,1)} %get-tuple-element.61), channel_id=1, source_target_pairs={{0,7},{1,6},{2,5},{3,4},{4,3},{5,2},{6,1},{7,0},{8,15},{9,14},{10,... | collective-permute-start | bytes 786440 | tf_op jit(solution)/shard_map/ppermute | solution.py:439
  101.4 24.7 %collective-permute-start.23 = (bf16[2,8,8,1024]{3,2,1,0:T(8,128)(2,1)}, bf16[2,8,8,1024]{3,2,1,0:T(8,128)(2,1)S(1)}, u32[]{:S(2)}, u32[]{:S(2)}) collective-permute-start(bf16[2,8,8,1024]{3,2,1,0:T(8,128)(2,1)} %get-tuple-element.64), channel_id=1, source_target_pairs={{0,14},{1,15},{2,12},{3,13},{4,10},{5,11},{6,8},{7,9},{8,6},{9,7},... | collective-permute-start | bytes 786440 | tf_op jit(solution)/shard_map/ppermute | solution.py:439
  101.5 31.0 %collective-permute-start.24 = (bf16[2,8,8,1024]{3,2,1,0:T(8,128)(2,1)S(1)}, bf16[2,8,8,1024]{3,2,1,0:T(8,128)(2,1)S(1)}, u32[]{:S(2)}, u32[]{:S(2)}) collective-permute-start(bf16[2,8,8,1024]{3,2,1,0:T(8,128)(2,1)S(1)} %copy-done.7), channel_id=1, source_target_pairs={{0,15},{1,14},{2,13},{3,12},{4,11},{5,10},{6,9},{7,8},{8,7},{9,6},... | collective-permute-start | bytes 786440 | tf_op jit(solution)/shard_map/ppermute | solution.py:439
  107.1 26.8 %collective-permute-start.9 = (bf16[1,27,8,128]{3,2,1,0:T(8,128)(2,1)S(1)}, bf16[1,27,8,128]{3,2,1,0:T(8,128)(2,1)S(1)}, u32[]{:S(2)}, u32[]{:S(2)}) collective-permute-start(bf16[1,27,8,128]{3,2,1,0:T(8,128)(2,1)S(1)} %get-tuple-element.44), channel_id=1, source_target_pairs={{0,8},{1,9},{2,10},{3,11},{4,12},{5,13},{6,14},{7,15},{8,0},{9,1},... | collective-permute-start | bytes 165896 | tf_op jit(solution)/shard_map/ppermute | solution.py:439
  132.5 1.4 %copy-start.2 = (bf16[25,8,128]{2,1,0:T(8,128)(2,1)S(1)}, bf16[25,8,128]{2,1,0:T(8,128)(2,1)}, u32[]{:S(2)}) copy-start(bf16[25,8,128]{2,1,0:T(8,128)(2,1)} %message.1) | copy-start | bytes 153604
  132.5 1.4 %copy-start.4 = (bf16[1,2,1024]{2,1,0:T(2,128)(2,1)S(1)}, bf16[1,2,1024]{2,1,0:T(2,128)(2,1)}, u32[]{:S(2)}) copy-start(bf16[1,2,1024]{2,1,0:T(2,128)(2,1)} %param.15) | copy-start | bytes 12292
  132.5 1.4 %copy-start.5 = (bf16[1,2,1024]{2,1,0:T(2,128)(2,1)S(1)}, bf16[1,2,1024]{2,1,0:T(2,128)(2,1)}, u32[]{:S(2)}) copy-start(bf16[1,2,1024]{2,1,0:T(2,128)(2,1)} %param.16) | copy-start | bytes 12292
where the time goes:
time: 137 us; the launch traced here: 135 us
  starting transfers between devices  57.5 us (42%)
  waiting for transfers between devices  46.1 us (34%)
  Pallas kernels  25.4 us (19%)
  local copies, waits for them, and re-layouts  3.72 us (3%)
  between operations  1.41 us (1%)
    ppermute x25, starting transfers between devices, swap(): lax.ppermute(array, 'seq', [(i, i ^ distance) for i in range(shards)])  57.5 us
    ppermute x25, waiting for transfers between devices, swap(): lax.ppermute(array, 'seq', [(i, i ^ distance) for i in range(shards)])  46.1 us
    pallas_call x1, Pallas kernels, attend(): pl.pallas_call(functools.partial(attend_kernel, rows_p, rows_d, capacity)...  7.49 us
    pallas_call x1, Pallas kernels, pack(): pl.pallas_call(functools.partial(pack_kernel, shards, capacity, partners)...  5.18 us
    pallas_call x3, Pallas kernels, fold(): pl.pallas_call(functools.partial(fold_kernel, rows), out_shape=(half, hal...  4.18 us
    pallas_call x3, Pallas kernels, settle(): pl.pallas_call(functools.partial(settle_kernel, partners, len(stores)), o...  3.48 us
    unnamed x16, local copies, waits for them, and re-layouts  3.12 us
  transfers between devices with their start and end apart: 25, of which 15 were waited for; matrix products, arithmetic and copies ran while one was open for 0% of the time, Pallas kernels for 11%

commit v1 on v0

--- a/solution.py
+++ b/solution.py
@@ -445,9 +445,10 @@
     plain, plain_side = [[k for k in group if not k & 2] for group in (upper, side)]
     other, other_side = [[k for k in group if k & 2] for group in (upper, side)]
     half = len(other) // 2
+    other = other[half:] + other[:half]
     first = plain[0]
-    opening = plain[1:2] + plain_side[: len(plain_side) // 2] + plain[2:3]
-    second = plain_side[len(plain_side) // 2 :] + plain[3:]
+    opening = plain_side[: len(plain_side) // 2] + plain[1:2]
+    second = plain_side[len(plain_side) // 2 :] + plain[2:]
     third = other[:half] + other_side
     return first, opening, second, third, [1, 2, 3], other[half:]
 
@@ -473,8 +474,9 @@
     pieces = {first: swap(piece, first)}
     message = make_message(prefill_q, decode_q, page_owner, context_len)
     far = {0: message}
-    for k in range(4, shards, 4):
-        far[k] = swap(message, k)
+    for bit in reversed(bits_of(shards)[2:]):
+        for k in list(far):
+            far[k | bit] = swap(far[k], bit)
     group = [0] + opening + second + third + near + last
     packed = pack(owners, page_counts, pages_k, pages_v, shards, capacity, group)
     for k, piece in zip(group, packed):

time: 137 us -> 151 us (1.10)
  the two profiles are of different devices: /device:TPU:13 before, /device:TPU:0 now
where the time goes in v1:
time: 151 us; the launch traced here: 150 us
  starting transfers between devices  65.9 us (44%)
  waiting for transfers between devices  53 us (35%)
  Pallas kernels  25.1 us (17%)
  local copies, waits for them, and re-layouts  3.72 us (2%)
    ppermute x25, starting transfers between devices, swap(): lax.ppermute(array, 'seq', [(i, i ^ distance) for i in range(shards)])  65.9 us
    ppermute x25, waiting for transfers between devices, swap(): lax.ppermute(array, 'seq', [(i, i ^ distance) for i in range(shards)])  53 us
    pallas_call x1, Pallas kernels, attend(): pl.pallas_call(functools.partial(attend_kernel, rows_p, rows_d, capacity)...  7.49 us
    pallas_call x1, Pallas kernels, pack(): pl.pallas_call(functools.partial(pack_kernel, shards, capacity, partners)...  4.94 us
    pallas_call x3, Pallas kernels, fold(): pl.pallas_call(functools.partial(fold_kernel, rows), out_shape=(half, hal...  4.18 us
    pallas_call x3, Pallas kernels, settle(): pl.pallas_call(functools.partial(settle_kernel, partners, len(stores)), o...  3.5 us
    unnamed x16, local copies, waits for them, and re-layouts  3.12 us
  transfers between devices with their start and end apart: 25, of which 12 were waited for; matrix products, arithmetic and copies ran while one was open for 0% of the time, Pallas kernels for 10%

profile of v1, /device:TPU:0, one launch (start us, length us, event | category | flops | bytes accessed | tf_op | source)
XLA Modules:
  0.0 150.1 jit_solution(5077291105841132917)
XLA Ops:
  1.3 1.5 message.1
  2.8 4.1 %collective-permute-start.1 = (bf16[25,8,128]{2,1,0:T(8,128)(2,1)}, bf16[25,8,128]{2,1,0:T(8,128)(2,1)S(1)}, u32[]{:S(2)}, u32[]{:S(2)}) collective-permute-start(bf16[25,8,128]{2,1,0:T(8,128)(2,1)} %message.1), channel_id=1, source_target_pairs={{0,8},{1,9},{2,10},{3,11},{4,12},{5,13},{6,14},{7,15},{8,0},{9,1},... | collective-permute-start | bytes 153608 | tf_op jit(solution)/shard_map/ppermute | solution.py:439
  6.8 1.6 %collective-permute-start = (bf16[25,8,128]{2,1,0:T(8,128)(2,1)}, bf16[25,8,128]{2,1,0:T(8,128)(2,1)S(1)}, u32[]{:S(2)}, u32[]{:S(2)}) collective-permute-start(bf16[25,8,128]{2,1,0:T(8,128)(2,1)} %message.1), channel_id=1, source_target_pairs={{0,4},{1,5},{2,6},{3,7},{4,0},{5,1},{6,2},{7,3},{8,12},{9,13},{10,... | collective-permute-start | bytes 153608 | tf_op jit(solution)/shard_map/ppermute | solution.py:439
  8.4 1.4 collective-permute-done.1
  9.8 1.3 collective-permute-start.2
  11.0 0.6 collective-permute-done
  11.6 2.3 %collective-permute-done.2 = bf16[25,8,128]{2,1,0:T(8,128)(2,1)S(1)} collective-permute-done((bf16[25,8,128]{2,1,0:T(8,128)(2,1)S(1)}, bf16[25,8,128]{2,1,0:T(8,128)(2,1)S(1)}, u32[]{:S(2)}, u32[]{:S(2)}) %collective-permute-start.2) | collective-permute-done | bytes 51232 | tf_op jit(solution)/shard_map/ppermute | solution.py:439
  13.9 0.8 pad_maximum_fusion.refs_0_
  14.7 1.8 %collective-permute-start.4 = (bf16[100,8,128]{2,1,0:T(8,128)(2,1)S(1)}, bf16[100,8,128]{2,1,0:T(8,128)(2,1)S(1)}, u32[]{:S(2)}, u32[]{:S(2)}) collective-permute-start(bf16[100,8,128]{2,1,0:T(8,128)(2,1)S(1)} %pad_maximum_fusion.refs_0_), channel_id=1, source_target_pairs={{0,2},{1,3},{2,0},{3,1},{4,6},{5,7},{6,4},{7,5},{8,10},{9,11},{10,... | collective-permute-start | bytes 614408 | tf_op jit(solution)/shard_map/ppermute | solution.py:439
  16.5 0.0 collective-permute-start.3
  16.5 4.0 %collective-permute-done.4.refs_2_ = bf16[100,8,128]{2,1,0:T(8,128)(2,1)S(1)} collective-permute-done((bf16[100,8,128]{2,1,0:T(8,128)(2,1)S(1)}, bf16[100,8,128]{2,1,0:T(8,128)(2,1)S(1)}, u32[]{:S(2)}, u32[]{:S(2)}) %collective-permute-start.4) | collective-permute-done | bytes 204832 | tf_op jit(solution)/shard_map/ppermute | solution.py:439
  20.5 0.0 collective-permute-start.5
  20.5 0.0 collective-permute-done.3.refs_1_
  20.6 1.4 collective-permute-done.5.refs_3_
  22.0 1.2 copy-done
  23.2 1.2 copy-done.1
  24.5 0.7 copy-done.6
  25.1 7.5 %attend.1 = (bf16[8,27,8,128]{3,2,1,0:T(8,128)(2,1)S(1)}, bf16[8,27,8,128]{3,2,1,0:T(8,128)(2,1)S(1)}, s32[16,128]{1,0:T(8,128)S(1)}) custom-call(s32[16]{0:T(128)S(1)} %copy-done.6, bf16[100,8,128]{2,1,0:T(8,128)(2,1)S(1)} %pad_maximum_fusion.refs_0_, bf16[100,8,128]{2,1,0:T(8,128)(2,1)S(1)} %collective-permute-done.3.refs_1_, ...), custom_call_target="tpu_custom_call" | custom-call | flops 805306368 | bytes 3670016 | tf_op jit(solution)/shard_map/attend/pallas_call | solution.py:266
  32.6 0.2 collective-permute-start.6
  32.8 4.9 %pack.1 = (bf16[2,8,8,1024]{3,2,1,0:T(8,128)(2,1)}, bf16[2,8,8,1024]{3,2,1,0:T(8,128)(2,1)}, bf16[2,8,8,1024]{3,2,1,0:T(8,128)(2,1)}, bf16[2,8,8,1024]{3,2,1,0:T...) custom-call(s32[64]{0:T(128)} %bitcast.24, ...), custom_call_target="tpu_custom_call" | custom-call | bytes 9961472 | tf_op jit(solution)/shard_map/pack/pallas_call | solution.py:97
  37.8 1.2 collective-permute-start.11
  39.0 2.6 %collective-permute-start.12 = (bf16[2,8,8,1024]{3,2,1,0:T(8,128)(2,1)}, bf16[2,8,8,1024]{3,2,1,0:T(8,128)(2,1)S(1)}, u32[]{:S(2)}, u32[]{:S(2)}) collective-permute-start(bf16[2,8,8,1024]{3,2,1,0:T(8,128)(2,1)} %get-tuple-element.49), channel_id=1, source_target_pairs={{0,9},{1,8},{2,11},{3,10},{4,13},{5,12},{6,15},{7,14},{8,1},{9,0},... | collective-permute-start | bytes 786440 | tf_op jit(solution)/shard_map/ppermute | solution.py:439
  41.6 0.9 collective-permute-start.13
  42.4 0.7 collective-permute-start.14
  43.1 0.0 collective-permute-done.6.got
  43.1 2.5 %collective-permute-start.15 = (bf16[2,8,8,1024]{3,2,1,0:T(8,128)(2,1)}, bf16[2,8,8,1024]{3,2,1,0:T(8,128)(2,1)S(1)}, u32[]{:S(2)}, u32[]{:S(2)}) collective-permute-start(bf16[2,8,8,1024]{3,2,1,0:T(8,128)(2,1)} %get-tuple-element.52), channel_id=1, source_target_pairs={{0,13},{1,12},{2,15},{3,14},{4,9},{5,8},{6,11},{7,10},{8,5},{9,4},... | collective-permute-start | bytes 786440 | tf_op jit(solution)/shard_map/ppermute | solution.py:439
  45.6 2.5 %fold.3 = (bf16[4,27,8,128]{3,2,1,0:T(8,128)(2,1)S(1)}, bf16[4,27,8,128]{3,2,1,0:T(8,128)(2,1)S(1)}) custom-call(bf16[8,27,8,128]{3,2,1,0:T(8,128)(2,1)S(1)} %get-tuple-element.37.keep, bf16[8,27,8,128]{3,2,1,0:T(8,128)(2,1)S(1)} %collective-permute-done.6.got), custom_call_target="tpu_custom_call" | custom-call | flops 884736 | bytes 1327104 | tf_op jit(solution)/shard_map/fold/pallas_call | solution.py:314
  48.2 4.6 %collective-permute-done.11.refs_2_ = bf16[2,8,8,1024]{3,2,1,0:T(8,128)(2,1)S(1)} collective-permute-done((bf16[2,8,8,1024]{3,2,1,0:T(8,128)(2,1)}, bf16[2,8,8,1024]{3,2,1,0:T(8,128)(2,1)S(1)}, u32[]{:S(2)}, u32[]{:S(2)}) %collective-permute-start.11) | collective-permute-done | bytes 262176 | tf_op jit(solution)/shard_map/ppermute | solution.py:439
  52.8 1.3 collective-permute-start.7
  54.1 0.0 collective-permute-done.12.refs_3_
  54.1 0.0 collective-permute-start.16
  54.1 3.6 %collective-permute-done.13.refs_4_ = bf16[2,8,8,1024]{3,2,1,0:T(8,128)(2,1)S(1)} collective-permute-done((bf16[2,8,8,1024]{3,2,1,0:T(8,128)(2,1)}, bf16[2,8,8,1024]{3,2,1,0:T(8,128)(2,1)S(1)}, u32[]{:S(2)}, u32[]{:S(2)}) %collective-permute-start.13) | collective-permute-done | bytes 262176 | tf_op jit(solution)/shard_map/ppermute | solution.py:439
  57.7 1.8 %collective-permute-start.17 = (bf16[2,8,8,1024]{3,2,1,0:T(8,128)(2,1)}, bf16[2,8,8,1024]{3,2,1,0:T(8,128)(2,1)S(1)}, u32[]{:S(2)}, u32[]{:S(2)}) collective-permute-start(bf16[2,8,8,1024]{3,2,1,0:T(8,128)(2,1)} %get-tuple-element.54), channel_id=1, source_target_pairs={{0,2},{1,3},{2,0},{3,1},{4,6},{5,7},{6,4},{7,5},{8,10},{9,11},{10,... | collective-permute-start | bytes 786440 | tf_op jit(solution)/shard_map/ppermute | solution.py:439
  59.6 6.9 %collective-permute-done.14.refs_5_ = bf16[2,8,8,1024]{3,2,1,0:T(8,128)(2,1)S(1)} collective-permute-done((bf16[2,8,8,1024]{3,2,1,0:T(8,128)(2,1)}, bf16[2,8,8,1024]{3,2,1,0:T(8,128)(2,1)S(1)}, u32[]{:S(2)}, u32[]{:S(2)}) %collective-permute-start.14) | collective-permute-done | bytes 262176 | tf_op jit(solution)/shard_map/ppermute | solution.py:439
  66.5 0.3 collective-permute-start.18
  66.8 2.5 %pick.1 = bf16[2,8,8,1024]{3,2,1,0:T(8,128)(2,1)} custom-call(s32[64]{0:T(128)} %bitcast.25, s32[16]{0:T(128)} %counts.5, bf16[64,8,1024]{2,1,0:T(8,128)(2,1)} %bitcast.14, bf16[64,8,1024]{2,1,0:T(8,128)(2,1)} %bitcast.16), custom_call_target="tpu_custom_call" | custom-call | bytes 524288 | tf_op jit(solution)/shard_map/pick/pallas_call | solution.py:154
  69.3 1.6 %collective-permute-done.15.refs_6_ = bf16[2,8,8,1024]{3,2,1,0:T(8,128)(2,1)S(1)} collective-permute-done((bf16[2,8,8,1024]{3,2,1,0:T(8,128)(2,1)}, bf16[2,8,8,1024]{3,2,1,0:T(8,128)(2,1)S(1)}, u32[]{:S(2)}, u32[]{:S(2)}) %collective-permute-start.15) | collective-permute-done | bytes 262176 | tf_op jit(solution)/shard_map/ppermute | solution.py:439
  70.9 8.0 %collective-permute-start.10 = (bf16[2,8,8,1024]{3,2,1,0:T(8,128)(2,1)}, bf16[2,8,8,1024]{3,2,1,0:T(8,128)(2,1)S(1)}, u32[]{:S(2)}, u32[]{:S(2)}) collective-permute-start(bf16[2,8,8,1024]{3,2,1,0:T(8,128)(2,1)} %pick.1), channel_id=1, source_target_pairs={{0,8},{1,9},{2,10},{3,11},{4,12},{5,13},{6,14},{7,15},{8,0},{9,1},... | collective-permute-start | bytes 786440 | tf_op jit(solution)/shard_map/ppermute | solution.py:439
  78.9 0.0 collective-permute-done.7.got
  78.9 1.5 collective-permute-start.19
  80.4 1.2 fold.4
  81.5 0.0 collective-permute-done.16.refs_7_
  81.6 0.1 collective-permute-start.8
  81.6 0.0 collective-permute-done.17.refs_8_
  81.6 2.7 %collective-permute-start.20 = (bf16[2,8,8,1024]{3,2,1,0:T(8,128)(2,1)}, bf16[2,8,8,1024]{3,2,1,0:T(8,128)(2,1)S(1)}, u32[]{:S(2)}, u32[]{:S(2)}) collective-permute-start(bf16[2,8,8,1024]{3,2,1,0:T(8,128)(2,1)} %get-tuple-element.59), channel_id=1, source_target_pairs={{0,15},{1,14},{2,13},{3,12},{4,11},{5,10},{6,9},{7,8},{8,7},{9,6},... | collective-permute-start | bytes 786440 | tf_op jit(solution)/shard_map/ppermute | solution.py:439
  84.4 0.0 collective-permute-done.18.refs_9_
  84.4 1.4 collective-permute-start.21
  85.8 17.4 %collective-permute-done.10.refs_1_ = bf16[2,8,8,1024]{3,2,1,0:T(8,128)(2,1)S(1)} collective-permute-done((bf16[2,8,8,1024]{3,2,1,0:T(8,128)(2,1)}, bf16[2,8,8,1024]{3,2,1,0:T(8,128)(2,1)S(1)}, u32[]{:S(2)}, u32[]{:S(2)}) %collective-permute-start.10) | collective-permute-done | bytes 262176 | tf_op jit(solution)/shard_map/ppermute | solution.py:439
  103.1 0.0 collective-permute-start.22
  103.1 0.0 collective-permute-done.19.refs_2_
  103.2 12.2 %collective-permute-start.23 = (bf16[2,8,8,1024]{3,2,1,0:T(8,128)(2,1)}, bf16[2,8,8,1024]{3,2,1,0:T(8,128)(2,1)S(1)}, u32[]{:S(2)}, u32[]{:S(2)}) collective-permute-start(bf16[2,8,8,1024]{3,2,1,0:T(8,128)(2,1)} %get-tuple-element.64), channel_id=1, source_target_pairs={{0,10},{1,11},{2,8},{3,9},{4,14},{5,15},{6,12},{7,13},{8,2},{9,3},... | collective-permute-start | bytes 786440 | tf_op jit(solution)/shard_map/ppermute | solution.py:439
  115.3 0.0 collective-permute-done.8.got
  115.3 0.0 collective-permute-start.24
  115.4 0.5 fold.5
  115.8 0.0 collective-permute-done.20.refs_3_
  115.8 19.8 %collective-permute-start.9 = (bf16[1,27,8,128]{3,2,1,0:T(8,128)(2,1)S(1)}, bf16[1,27,8,128]{3,2,1,0:T(8,128)(2,1)S(1)}, u32[]{:S(2)}, u32[]{:S(2)}) collective-permute-start(bf16[1,27,8,128]{3,2,1,0:T(8,128)(2,1)S(1)} %get-tuple-element.44), channel_id=1, source_target_pairs={{0,8},{1,9},{2,10},{3,11},{4,12},{5,13},{6,14},{7,15},{8,0},{9,1},... | collective-permute-start | bytes 165896 | tf_op jit(solution)/shard_map/ppermute | solution.py:439
  135.6 1.6 %settle.3 = (bf16[16,8,8,1024]{3,2,1,0:T(8,128)(2,1)}, bf16[16,8,8,1024]{3,2,1,0:T(8,128)(2,1)}) custom-call(bf16[2,8,8,1024]{3,2,1,0:T(8,128)(2,1)S(1)} %copy-done.3, bf16[2,8,8,1024]{3,2,1,0:T(8,128)(2,1)S(1)} %collective-permute-done.10.refs_1_, bf16[2,8,8,1024]{3,2,1,0:T(8,128)(2,1)S(1)} %collective-permute-done.11.refs_2_, ...), custom_call_target="tpu_custom_call" | custom-call | bytes 5242880 | tf_op jit(solution)/shard_map/settle/pallas_call | solution.py:349
  137.3 0.0 collective-permute-done.21.refs_4_
  137.3 1.0 settle.4
  138.3 3.7 %collective-permute-done.23.refs_2_ = bf16[2,8,8,1024]{3,2,1,0:T(8,128)(2,1)S(1)} collective-permute-done((bf16[2,8,8,1024]{3,2,1,0:T(8,128)(2,1)}, bf16[2,8,8,1024]{3,2,1,0:T(8,128)(2,1)S(1)}, u32[]{:S(2)}, u32[]{:S(2)}) %collective-permute-start.23) | collective-permute-done | bytes 262176 | tf_op jit(solution)/shard_map/ppermute | solution.py:439
  142.0 5.6 %collective-permute-done.24.refs_3_ = bf16[2,8,8,1024]{3,2,1,0:T(8,128)(2,1)S(1)} collective-permute-done((bf16[2,8,8,1024]{3,2,1,0:T(8,128)(2,1)S(1)}, bf16[2,8,8,1024]{3,2,1,0:T(8,128)(2,1)S(1)}, u32[]{:S(2)}, u32[]{:S(2)}) %collective-permute-start.24) | collective-permute-done | bytes 262176 | tf_op jit(solution)/shard_map/ppermute | solution.py:439
  147.6 0.8 settle.5
  148.4 0.6 reshape.57
  149.0 1.1 merge.1
  (15 shorter events, 0.0 us)
Async XLA Ops:
  2.8 7.0 %collective-permute-start.1 = (bf16[25,8,128]{2,1,0:T(8,128)(2,1)}, bf16[25,8,128]{2,1,0:T(8,128)(2,1)S(1)}, u32[]{:S(2)}, u32[]{:S(2)}) collective-permute-start(bf16[25,8,128]{2,1,0:T(8,128)(2,1)} %message.1), channel_id=1, source_target_pairs={{0,8},{1,9},{2,10},{3,11},{4,12},{5,13},{6,14},{7,15},{8,0},{9,1},... | collective-permute-start | bytes 153608 | tf_op jit(solution)/shard_map/ppermute | solution.py:439
  6.8 4.8 %collective-permute-start = (bf16[25,8,128]{2,1,0:T(8,128)(2,1)}, bf16[25,8,128]{2,1,0:T(8,128)(2,1)S(1)}, u32[]{:S(2)}, u32[]{:S(2)}) collective-permute-start(bf16[25,8,128]{2,1,0:T(8,128)(2,1)} %message.1), channel_id=1, source_target_pairs={{0,4},{1,5},{2,6},{3,7},{4,0},{5,1},{6,2},{7,3},{8,12},{9,13},{10,... | collective-permute-start | bytes 153608 | tf_op jit(solution)/shard_map/ppermute | solution.py:439
  9.8 4.1 %collective-permute-start.2 = (bf16[25,8,128]{2,1,0:T(8,128)(2,1)S(1)}, bf16[25,8,128]{2,1,0:T(8,128)(2,1)S(1)}, u32[]{:S(2)}, u32[]{:S(2)}) collective-permute-start(bf16[25,8,128]{2,1,0:T(8,128)(2,1)S(1)} %collective-permute-done.1), channel_id=1, source_target_pairs={{0,4},{1,5},{2,6},{3,7},{4,0},{5,1},{6,2},{7,3},{8,12},{9,13},{10,... | collective-permute-start | bytes 153608 | tf_op jit(solution)/shard_map/ppermute | solution.py:439
  14.7 5.8 %collective-permute-start.4 = (bf16[100,8,128]{2,1,0:T(8,128)(2,1)S(1)}, bf16[100,8,128]{2,1,0:T(8,128)(2,1)S(1)}, u32[]{:S(2)}, u32[]{:S(2)}) collective-permute-start(bf16[100,8,128]{2,1,0:T(8,128)(2,1)S(1)} %pad_maximum_fusion.refs_0_), channel_id=1, source_target_pairs={{0,2},{1,3},{2,0},{3,1},{4,6},{5,7},{6,4},{7,5},{8,10},{9,11},{10,... | collective-permute-start | bytes 614408 | tf_op jit(solution)/shard_map/ppermute | solution.py:439
  16.5 4.0 %collective-permute-start.3 = (bf16[100,8,128]{2,1,0:T(8,128)(2,1)S(1)}, bf16[100,8,128]{2,1,0:T(8,128)(2,1)S(1)}, u32[]{:S(2)}, u32[]{:S(2)}) collective-permute-start(bf16[100,8,128]{2,1,0:T(8,128)(2,1)S(1)} %pad_maximum_fusion.refs_0_), channel_id=1, source_target_pairs={{0,1},{1,0},{2,3},{3,2},{4,5},{5,4},{6,7},{7,6},{8,9},{9,8},{10,11... | collective-permute-start | bytes 614408 | tf_op jit(solution)/shard_map/ppermute | solution.py:439
  20.5 1.5 collective-permute-start.5
  22.0 1.2 copy-start
  23.2 1.2 copy-start.1
  24.5 0.7 copy-start.6
  32.6 10.5 %collective-permute-start.6 = (bf16[8,27,8,128]{3,2,1,0:T(8,128)(2,1)S(1)}, bf16[8,27,8,128]{3,2,1,0:T(8,128)(2,1)S(1)}, u32[]{:S(2)}, u32[]{:S(2)}) collective-permute-start(bf16[8,27,8,128]{3,2,1,0:T(8,128)(2,1)S(1)} %get-tuple-element.38), channel_id=1, source_target_pairs={{0,1},{1,0},{2,3},{3,2},{4,5},{5,4},{6,7},{7,6},{8,9},{9,8},{10,11... | collective-permute-start | bytes 1327112 | tf_op jit(solution)/shard_map/ppermute | solution.py:439
  37.7 77.6 %copy-start.7 = (bf16[2,8,8,1024]{3,2,1,0:T(8,128)(2,1)S(1)}, bf16[2,8,8,1024]{3,2,1,0:T(8,128)(2,1)}, u32[]{:S(2)}) copy-start(bf16[2,8,8,1024]{3,2,1,0:T(8,128)(2,1)} %get-tuple-element.65) | copy-start | bytes 786436
  37.7 97.9 %copy-start.3 = (bf16[2,8,8,1024]{3,2,1,0:T(8,128)(2,1)S(1)}, bf16[2,8,8,1024]{3,2,1,0:T(8,128)(2,1)}, u32[]{:S(2)}) copy-start(bf16[2,8,8,1024]{3,2,1,0:T(8,128)(2,1)} %get-tuple-element.47.refs_0_) | copy-start | bytes 786436
  37.8 15.0 %collective-permute-start.11 = (bf16[2,8,8,1024]{3,2,1,0:T(8,128)(2,1)}, bf16[2,8,8,1024]{3,2,1,0:T(8,128)(2,1)S(1)}, u32[]{:S(2)}, u32[]{:S(2)}) collective-permute-start(bf16[2,8,8,1024]{3,2,1,0:T(8,128)(2,1)} %get-tuple-element.48), channel_id=1, source_target_pairs={{0,4},{1,5},{2,6},{3,7},{4,0},{5,1},{6,2},{7,3},{8,12},{9,13},{10,... | collective-permute-start | bytes 786440 | tf_op jit(solution)/shard_map/ppermute | solution.py:439
  39.0 15.1 %collective-permute-start.12 = (bf16[2,8,8,1024]{3,2,1,0:T(8,128)(2,1)}, bf16[2,8,8,1024]{3,2,1,0:T(8,128)(2,1)S(1)}, u32[]{:S(2)}, u32[]{:S(2)}) collective-permute-start(bf16[2,8,8,1024]{3,2,1,0:T(8,128)(2,1)} %get-tuple-element.49), channel_id=1, source_target_pairs={{0,9},{1,8},{2,11},{3,10},{4,13},{5,12},{6,15},{7,14},{8,1},{9,0},... | collective-permute-start | bytes 786440 | tf_op jit(solution)/shard_map/ppermute | solution.py:439
  41.6 16.2 %collective-permute-start.13 = (bf16[2,8,8,1024]{3,2,1,0:T(8,128)(2,1)}, bf16[2,8,8,1024]{3,2,1,0:T(8,128)(2,1)S(1)}, u32[]{:S(2)}, u32[]{:S(2)}) collective-permute-start(bf16[2,8,8,1024]{3,2,1,0:T(8,128)(2,1)} %get-tuple-element.50), channel_id=1, source_target_pairs={{0,5},{1,4},{2,7},{3,6},{4,1},{5,0},{6,3},{7,2},{8,13},{9,12},{10,... | collective-permute-start | bytes 786440 | tf_op jit(solution)/shard_map/ppermute | solution.py:439
  42.4 24.1 %collective-permute-start.14 = (bf16[2,8,8,1024]{3,2,1,0:T(8,128)(2,1)}, bf16[2,8,8,1024]{3,2,1,0:T(8,128)(2,1)S(1)}, u32[]{:S(2)}, u32[]{:S(2)}) collective-permute-start(bf16[2,8,8,1024]{3,2,1,0:T(8,128)(2,1)} %get-tuple-element.51), channel_id=1, source_target_pairs={{0,12},{1,13},{2,14},{3,15},{4,8},{5,9},{6,10},{7,11},{8,4},{9,5},... | collective-permute-start | bytes 786440 | tf_op jit(solution)/shard_map/ppermute | solution.py:439
  43.1 27.8 %collective-permute-start.15 = (bf16[2,8,8,1024]{3,2,1,0:T(8,128)(2,1)}, bf16[2,8,8,1024]{3,2,1,0:T(8,128)(2,1)S(1)}, u32[]{:S(2)}, u32[]{:S(2)}) collective-permute-start(bf16[2,8,8,1024]{3,2,1,0:T(8,128)(2,1)} %get-tuple-element.52), channel_id=1, source_target_pairs={{0,13},{1,12},{2,15},{3,14},{4,9},{5,8},{6,11},{7,10},{8,5},{9,4},... | collective-permute-start | bytes 786440 | tf_op jit(solution)/shard_map/ppermute | solution.py:439
  52.8 26.1 %collective-permute-start.7 = (bf16[4,27,8,128]{3,2,1,0:T(8,128)(2,1)S(1)}, bf16[4,27,8,128]{3,2,1,0:T(8,128)(2,1)S(1)}, u32[]{:S(2)}, u32[]{:S(2)}) collective-permute-start(bf16[4,27,8,128]{3,2,1,0:T(8,128)(2,1)S(1)} %get-tuple-element.40), channel_id=1, source_target_pairs={{0,2},{1,3},{2,0},{3,1},{4,6},{5,7},{6,4},{7,5},{8,10},{9,11},{10,... | collective-permute-start | bytes 663560 | tf_op jit(solution)/shard_map/ppermute | solution.py:439
  54.1 27.4 %collective-permute-start.16 = (bf16[2,8,8,1024]{3,2,1,0:T(8,128)(2,1)}, bf16[2,8,8,1024]{3,2,1,0:T(8,128)(2,1)S(1)}, u32[]{:S(2)}, u32[]{:S(2)}) collective-permute-start(bf16[2,8,8,1024]{3,2,1,0:T(8,128)(2,1)} %get-tuple-element.53), channel_id=1, source_target_pairs={{0,1},{1,0},{2,3},{3,2},{4,5},{5,4},{6,7},{7,6},{8,9},{9,8},{10,11... | collective-permute-start | bytes 786440 | tf_op jit(solution)/shard_map/ppermute | solution.py:439
  57.7 23.9 %collective-permute-start.17 = (bf16[2,8,8,1024]{3,2,1,0:T(8,128)(2,1)}, bf16[2,8,8,1024]{3,2,1,0:T(8,128)(2,1)S(1)}, u32[]{:S(2)}, u32[]{:S(2)}) collective-permute-start(bf16[2,8,8,1024]{3,2,1,0:T(8,128)(2,1)} %get-tuple-element.54), channel_id=1, source_target_pairs={{0,2},{1,3},{2,0},{3,1},{4,6},{5,7},{6,4},{7,5},{8,10},{9,11},{10,... | collective-permute-start | bytes 786440 | tf_op jit(solution)/shard_map/ppermute | solution.py:439
  66.5 17.9 %collective-permute-start.18 = (bf16[2,8,8,1024]{3,2,1,0:T(8,128)(2,1)}, bf16[2,8,8,1024]{3,2,1,0:T(8,128)(2,1)S(1)}, u32[]{:S(2)}, u32[]{:S(2)}) collective-permute-start(bf16[2,8,8,1024]{3,2,1,0:T(8,128)(2,1)} %get-tuple-element.55), channel_id=1, source_target_pairs={{0,3},{1,2},{2,1},{3,0},{4,7},{5,6},{6,5},{7,4},{8,11},{9,10},{10,... | collective-permute-start | bytes 786440 | tf_op jit(solution)/shard_map/ppermute | solution.py:439
  70.9 32.3 %collective-permute-start.10 = (bf16[2,8,8,1024]{3,2,1,0:T(8,128)(2,1)}, bf16[2,8,8,1024]{3,2,1,0:T(8,128)(2,1)S(1)}, u32[]{:S(2)}, u32[]{:S(2)}) collective-permute-start(bf16[2,8,8,1024]{3,2,1,0:T(8,128)(2,1)} %pick.1), channel_id=1, source_target_pairs={{0,8},{1,9},{2,10},{3,11},{4,12},{5,13},{6,14},{7,15},{8,0},{9,1},... | collective-permute-start | bytes 786440 | tf_op jit(solution)/shard_map/ppermute | solution.py:439
  78.9 24.3 %collective-permute-start.19 = (bf16[2,8,8,1024]{3,2,1,0:T(8,128)(2,1)}, bf16[2,8,8,1024]{3,2,1,0:T(8,128)(2,1)S(1)}, u32[]{:S(2)}, u32[]{:S(2)}) collective-permute-start(bf16[2,8,8,1024]{3,2,1,0:T(8,128)(2,1)} %get-tuple-element.58), channel_id=1, source_target_pairs={{0,14},{1,15},{2,12},{3,13},{4,10},{5,11},{6,8},{7,9},{8,6},{9,7},... | collective-permute-start | bytes 786440 | tf_op jit(solution)/shard_map/ppermute | solution.py:439
  81.6 33.8 %collective-permute-start.8 = (bf16[2,27,8,128]{3,2,1,0:T(8,128)(2,1)S(1)}, bf16[2,27,8,128]{3,2,1,0:T(8,128)(2,1)S(1)}, u32[]{:S(2)}, u32[]{:S(2)}) collective-permute-start(bf16[2,27,8,128]{3,2,1,0:T(8,128)(2,1)S(1)} %get-tuple-element.42), channel_id=1, source_target_pairs={{0,4},{1,5},{2,6},{3,7},{4,0},{5,1},{6,2},{7,3},{8,12},{9,13},{10,... | collective-permute-start | bytes 331784 | tf_op jit(solution)/shard_map/ppermute | solution.py:439
  81.6 34.2 %collective-permute-start.20 = (bf16[2,8,8,1024]{3,2,1,0:T(8,128)(2,1)}, bf16[2,8,8,1024]{3,2,1,0:T(8,128)(2,1)S(1)}, u32[]{:S(2)}, u32[]{:S(2)}) collective-permute-start(bf16[2,8,8,1024]{3,2,1,0:T(8,128)(2,1)} %get-tuple-element.59), channel_id=1, source_target_pairs={{0,15},{1,14},{2,13},{3,12},{4,11},{5,10},{6,9},{7,8},{8,7},{9,6},... | collective-permute-start | bytes 786440 | tf_op jit(solution)/shard_map/ppermute | solution.py:439
  84.4 52.9 %collective-permute-start.21 = (bf16[2,8,8,1024]{3,2,1,0:T(8,128)(2,1)}, bf16[2,8,8,1024]{3,2,1,0:T(8,128)(2,1)S(1)}, u32[]{:S(2)}, u32[]{:S(2)}) collective-permute-start(bf16[2,8,8,1024]{3,2,1,0:T(8,128)(2,1)} %get-tuple-element.60), channel_id=1, source_target_pairs={{0,6},{1,7},{2,4},{3,5},{4,2},{5,3},{6,0},{7,1},{8,14},{9,15},{10,... | collective-permute-start | bytes 786440 | tf_op jit(solution)/shard_map/ppermute | solution.py:439
  103.1 34.1 %collective-permute-start.22 = (bf16[2,8,8,1024]{3,2,1,0:T(8,128)(2,1)}, bf16[2,8,8,1024]{3,2,1,0:T(8,128)(2,1)S(1)}, u32[]{:S(2)}, u32[]{:S(2)}) collective-permute-start(bf16[2,8,8,1024]{3,2,1,0:T(8,128)(2,1)} %get-tuple-element.61), channel_id=1, source_target_pairs={{0,7},{1,6},{2,5},{3,4},{4,3},{5,2},{6,1},{7,0},{8,15},{9,14},{10,... | collective-permute-start | bytes 786440 | tf_op jit(solution)/shard_map/ppermute | solution.py:439
  103.2 38.8 %collective-permute-start.23 = (bf16[2,8,8,1024]{3,2,1,0:T(8,128)(2,1)}, bf16[2,8,8,1024]{3,2,1,0:T(8,128)(2,1)S(1)}, u32[]{:S(2)}, u32[]{:S(2)}) collective-permute-start(bf16[2,8,8,1024]{3,2,1,0:T(8,128)(2,1)} %get-tuple-element.64), channel_id=1, source_target_pairs={{0,10},{1,11},{2,8},{3,9},{4,14},{5,15},{6,12},{7,13},{8,2},{9,3},... | collective-permute-start | bytes 786440 | tf_op jit(solution)/shard_map/ppermute | solution.py:439
  115.3 32.2 %collective-permute-start.24 = (bf16[2,8,8,1024]{3,2,1,0:T(8,128)(2,1)S(1)}, bf16[2,8,8,1024]{3,2,1,0:T(8,128)(2,1)S(1)}, u32[]{:S(2)}, u32[]{:S(2)}) collective-permute-start(bf16[2,8,8,1024]{3,2,1,0:T(8,128)(2,1)S(1)} %copy-done.7), channel_id=1, source_target_pairs={{0,11},{1,10},{2,9},{3,8},{4,15},{5,14},{6,13},{7,12},{8,3},{9,2},... | collective-permute-start | bytes 786440 | tf_op jit(solution)/shard_map/ppermute | solution.py:439
  115.8 33.2 %collective-permute-start.9 = (bf16[1,27,8,128]{3,2,1,0:T(8,128)(2,1)S(1)}, bf16[1,27,8,128]{3,2,1,0:T(8,128)(2,1)S(1)}, u32[]{:S(2)}, u32[]{:S(2)}) collective-permute-start(bf16[1,27,8,128]{3,2,1,0:T(8,128)(2,1)S(1)} %get-tuple-element.44), channel_id=1, source_target_pairs={{0,8},{1,9},{2,10},{3,11},{4,12},{5,13},{6,14},{7,15},{8,0},{9,1},... | collective-permute-start | bytes 165896 | tf_op jit(solution)/shard_map/ppermute | solution.py:439
  147.6 1.4 copy-start.2
  147.6 1.4 copy-start.4
  147.6 1.4 copy-start.5
